TPU v7x, 256 devices: a whole 4x4x8 slice. The times are simulated.
256 devices in a mesh: seq: 16 (over y, x), head: 16 (over z, core).
Axes of the slice: x: 4, y: 4, z: 8, core: 2. Of those that a mesh axis runs over, the one named last changes fastest.
Arguments:
- query_key: bfloat16 [2, 16384, 2048], P(None, 'seq', 'head'), may hold values from -6 to 6
- values: bfloat16 [2, 16384, 2048], P(None, 'seq', 'head'), may hold values from -6 to 6
- out_gate: bfloat16 [2, 16384, 2048], P(None, 'seq', 'head'), may hold values from -6 to 6
- log_gate: float32 [2, 16, 16384], P(None, 'head', 'seq'), may hold values from -1.3 to 0, as said below
- strength: float32 [2, 16, 16384], P(None, 'head', 'seq'), may hold values from 0 to 1, as said below
- norm_gain: float32 [128], replicated, may hold values from 0.1 to 1.9
Outputs:
- head_outputs: bfloat16 [2, 16384, 2048], P(None, 'seq', 'head')
Inputs may be any that keep to these rules, and one draw needn't show every extreme that they name: log_gate is the natural logarithm of a per-token decay factor of each head's state. strength is the per-token write strength of each head.
All inputs are finite; a program needn't handle non-finite values.
Results may differ from a plain program's by a relative error of at most 0.001.
Values may be sent and summed in bfloat16 or wider, within the bound.
A program may use at most 64 MiB of HBM per device.

v0:
```python
from functools import partial

import jax
import jax.numpy as jnp
from jax import lax
from jax.sharding import PartitionSpec as P

GROUP = 64


def from_partner(block, axis, bit):
    count = lax.axis_size(axis)
    route = []
    for low in range(count):
        high = low | 1 << bit
        if high != low and high < count:
            route += [(low, high), (high, low)]
    return lax.ppermute(block, axis, route)


def from_behind(block, axis, distance):
    devices = range(lax.axis_size(axis))
    route = [(i - distance, i) for i in devices if i - distance in devices]
    return lax.ppermute(block, axis, route)


def mult(form, left, right):
    return jnp.einsum(form, left, right, precision=lax.Precision.HIGHEST)


def normalize(vectors):
    return vectors / jnp.sqrt(jnp.sum(vectors * vectors, axis=-1, keepdims=True) + 1e-06)


def solve_lower(system, right_side):
    leading = system.shape[:-2]
    flat_sys = system.reshape((-1,) + system.shape[-2:])
    flat_rhs = right_side.reshape((-1,) + right_side.shape[-2:])
    solver = partial(jax.scipy.linalg.solve_triangular, lower=True, unit_diagonal=True)
    solved = jax.vmap(solver)(flat_sys, flat_rhs)
    return solved.reshape(leading + solved.shape[-2:])


def group_terms(queries, keys, vals, log_steps, writes):
    span = log_steps.shape[-1]
    cumulative = jnp.cumsum(log_steps, axis=-1)
    token_places = jnp.arange(span)
    causal = token_places[:, None] >= token_places[None, :]
    strict = token_places[:, None] > token_places[None, :]
    spread = cumulative[..., :, None] - cumulative[..., None, :]
    decays = jnp.where(causal, jnp.exp(jnp.where(causal, spread, 0.0)), 0.0)
    key_gram = mult("...td,...sd->...ts", keys, keys)
    lower_part = jnp.where(strict, decays * key_gram * writes[..., None, :], 0.0)
    system = lower_part + jnp.eye(span, dtype=jnp.float32)
    growth = jnp.exp(cumulative)
    right_side = jnp.concatenate([vals, growth[..., None] * keys], axis=-1)
    solved = solve_lower(system, right_side)
    val_width = vals.shape[-1]
    fresh_vals = solved[..., :val_width]
    key_mix = solved[..., val_width:]
    mixing = jnp.where(
        causal, decays * mult("...td,...sd->...ts", queries, keys) * writes[..., None, :], 0.0
    )
    query_lead = growth[..., None] * queries
    key_tail = keys * (jnp.exp(cumulative[..., -1:] - cumulative) * writes)[..., None]
    group_decay = growth[..., -1]
    return (fresh_vals, key_mix, mixing, query_lead, key_tail, group_decay)


def gated_norm(raw, out_gate, norm_gain):
    mean_square = jnp.mean(raw * raw, axis=-1, keepdims=True)
    gate_val = out_gate.astype(jnp.float32)
    scaled = raw / jnp.sqrt(mean_square + 1e-06) * norm_gain
    return (scaled * gate_val * jax.nn.sigmoid(gate_val)).astype(jnp.bfloat16)


def advance_outputs(state, inputs):
    fresh_vals, key_mix, mixing, query_lead, key_tail, group_decay = inputs
    update = fresh_vals - mult("bcd,bde->bce", key_mix, state)
    output = mult("bcd,bde->bce", query_lead, state) + mult("bcs,bse->bce", mixing, update)
    new_state = group_decay[:, None, None] * state + mult("bcd,bce->bde", key_tail, update)
    return (new_state, output)


def body(query_key, values, out_gate, log_gate, strength, norm_gain):
    partner = from_partner(query_key, "head", 0)
    is_query = lax.axis_index("head") % 2 == 0
    queries = normalize(jnp.where(is_query, query_key, partner).astype(jnp.float32))
    keys = normalize(jnp.where(is_query, partner, query_key).astype(jnp.float32))
    requests, length, val_width = values.shape
    key_width = keys.shape[-1]
    num_blocks = length // GROUP

    def blocks(array):
        return array.reshape(requests, num_blocks, GROUP, array.shape[-1])

    log_steps = log_gate[:, 0, :].reshape(requests, num_blocks, GROUP)
    writes = strength[:, 0, :].reshape(requests, num_blocks, GROUP)
    terms = group_terms(
        blocks(queries), blocks(keys), blocks(values.astype(jnp.float32)), log_steps, writes
    )
    stacked = jax.tree.map(lambda array: jnp.moveaxis(array, 1, 0), terms)
    local_start = jnp.zeros((requests, key_width, val_width), jnp.float32)
    identity_mat = jnp.broadcast_to(
        jnp.eye(key_width, dtype=jnp.float32), (requests, key_width, key_width)
    )

    def first_step(state_pair, inputs):
        local_state, transfer = state_pair
        fresh_vals, key_mix, mixing, query_lead, key_tail, group_decay = inputs
        update = fresh_vals - mult("bcd,bde->bce", key_mix, local_state)
        new_local = group_decay[:, None, None] * local_state + mult(
            "bcd,bce->bde", key_tail, update
        )
        moved = mult("bcd,bde->bce", key_mix, transfer)
        new_transfer = group_decay[:, None, None] * transfer - mult("bcd,bce->bde", key_tail, moved)
        return ((new_local, new_transfer), None)

    final_pair, unused_out = lax.scan(first_step, (local_start, identity_mat), stacked)
    local_end, transfer_end = final_pair

    def relay_step(turn_idx, received):
        passed = mult("bij,bjk->bik", transfer_end, received) + local_end
        return from_behind(passed, "seq", 1)

    incoming = lax.fori_loop(0, lax.axis_size("seq") - 1, relay_step, local_start)
    last_state, raw = lax.scan(advance_outputs, incoming, stacked)
    raw = jnp.moveaxis(raw, 0, 1).reshape(requests, length, val_width)
    return gated_norm(raw, out_gate, norm_gain)


def solution(mesh):
    return jax.shard_map(
        body,
        mesh=mesh,
        in_specs=(
            P(None, "seq", "head"),
            P(None, "seq", "head"),
            P(None, "seq", "head"),
            P(None, "head", "seq"),
            P(None, "head", "seq"),
            P(),
        ),
        out_specs=P(None, "seq", "head"),
        check_vma=False,
    )
```

profile of v0, /device:TPU:56, one launch (start us, length us, event | category | flops | bytes accessed | tf_op | source)
XLA Modules:
  0.0 374.9 jit_solution(17256501815293321902)
XLA Ops:
  2.3 2.2 convert.4
  8.2 2.0 copy.55
  10.2 4.4 %select_add_fusion = f32[32,1,64,64]{0,3,2,1:T(8,128)} fusion(f32[32,1,64,64]{0,3,2,1:T(8,128)} %copy.55, f32[64,64]{1,0:T(8,128)S(1)} %get-tuple-element.273, pred[64,64]{1,0:T(8,128)(4,1)S(1)} %get-tuple-element.272), kind=kLoop, calls=%fused_computation.47 | loop fusion | flops 262144 | bytes 1069056 | tf_op jit(solution)/shard_map/vmap(jit(_solve_triangular))/triangular_solve | solution.py:40
  14.6 68.5 %custom-call.4 = f32[32,1,64,64]{0,2,3,1:T(8,128)} custom-call(f32[32,1,64,64]{0,3,2,1:T(8,128)} %select_add_fusion), custom_call_target="InvertDiagBlocksLowerTriangular" | custom-call | tf_op jit(solution)/shard_map/vmap(jit(_solve_triangular))/triangular_solve | solution.py:40
  83.1 2.9 copy.56
  87.2 1.9 fusion.34
  92.1 62.0 %while.37 = (s32[]{:T(128)}, f32[2,128,128]{2,1,0:T(8,128)S(1)}, f32[2,128,128]{2,1,0:T(8,128)S(1)}, f32[16,2]{1,0:T(8,128)S(1)}, f32[16,2,64,128]{3,2,1,0:T(8,1...) while((s32[]{:T(128)}, f32[2,128,128]{2,1,0:T(8,128)S(1)}, ...), condition=%wide.region_3.4_spmd.clone, body=%wide.region_2.3_spmd.clone.sunk | while | flops 100876288 | bytes 1378448 | solution.py:119
  155.5 2.8 fusion.43
  158.3 141.6 %while.35 = (s32[]{:T(128)}, f32[2,128,128]{2,1,0:T(8,128)S(1)}, f32[2,128,128]{2,1,0:T(8,128)S(1)}, f32[2,128,128]{2,1,0:T(8,128)S(1)}, s32[]{:T(128)}) while((s32[]{:T(128)}, f32[2,128,128]{2,1,0:T(8,128)S(1)}, f32[2,128,128]{2,1,0:T(8,128)S(1)}, f32[2,128,128]{2,1,0:T(8,128)S(1)}, s32[]{:T(128)}) %tuple.68), condition=%wide.region_5.6_spmd, body=%wide.region_4.5_spmd.sunk | while | flops 50364416 | bytes 1048677 | solution.py:126
  158.6 3.4 collective-permute-start
  162.0 6.5 %collective-permute-done = f32[2,128,128]{2,1,0:T(8,128)S(1)} collective-permute-done((f32[2,128,128]{2,1,0:T(8,128)S(1)}, f32[2,128,128]{2,1,0:T(8,128)S(1)}, u32[]{:S(2)}, u32[]{:S(2)}) %collective-permute-start) | collective-permute-done | bytes 131104 | tf_op jit(solution)/shard_map/while/body/eval_jaxpr/ppermute | solution.py:24
  168.7 1.9 collective-permute-start
  170.7 7.1 %collective-permute-done = f32[2,128,128]{2,1,0:T(8,128)S(1)} collective-permute-done((f32[2,128,128]{2,1,0:T(8,128)S(1)}, f32[2,128,128]{2,1,0:T(8,128)S(1)}, u32[]{:S(2)}, u32[]{:S(2)}) %collective-permute-start) | collective-permute-done | bytes 131104 | tf_op jit(solution)/shard_map/while/body/eval_jaxpr/ppermute | solution.py:24
  178.0 1.9 collective-permute-start
  180.0 7.0 %collective-permute-done = f32[2,128,128]{2,1,0:T(8,128)S(1)} collective-permute-done((f32[2,128,128]{2,1,0:T(8,128)S(1)}, f32[2,128,128]{2,1,0:T(8,128)S(1)}, u32[]{:S(2)}, u32[]{:S(2)}) %collective-permute-start) | collective-permute-done | bytes 131104 | tf_op jit(solution)/shard_map/while/body/eval_jaxpr/ppermute | solution.py:24
  187.3 1.9 collective-permute-start
  189.2 7.0 %collective-permute-done = f32[2,128,128]{2,1,0:T(8,128)S(1)} collective-permute-done((f32[2,128,128]{2,1,0:T(8,128)S(1)}, f32[2,128,128]{2,1,0:T(8,128)S(1)}, u32[]{:S(2)}, u32[]{:S(2)}) %collective-permute-start) | collective-permute-done | bytes 131104 | tf_op jit(solution)/shard_map/while/body/eval_jaxpr/ppermute | solution.py:24
  198.5 7.0 %collective-permute-done = f32[2,128,128]{2,1,0:T(8,128)S(1)} collective-permute-done((f32[2,128,128]{2,1,0:T(8,128)S(1)}, f32[2,128,128]{2,1,0:T(8,128)S(1)}, u32[]{:S(2)}, u32[]{:S(2)}) %collective-permute-start) | collective-permute-done | bytes 131104 | tf_op jit(solution)/shard_map/while/body/eval_jaxpr/ppermute | solution.py:24
  207.7 7.0 %collective-permute-done = f32[2,128,128]{2,1,0:T(8,128)S(1)} collective-permute-done((f32[2,128,128]{2,1,0:T(8,128)S(1)}, f32[2,128,128]{2,1,0:T(8,128)S(1)}, u32[]{:S(2)}, u32[]{:S(2)}) %collective-permute-start) | collective-permute-done | bytes 131104 | tf_op jit(solution)/shard_map/while/body/eval_jaxpr/ppermute | solution.py:24
  216.9 7.2 %collective-permute-done = f32[2,128,128]{2,1,0:T(8,128)S(1)} collective-permute-done((f32[2,128,128]{2,1,0:T(8,128)S(1)}, f32[2,128,128]{2,1,0:T(8,128)S(1)}, u32[]{:S(2)}, u32[]{:S(2)}) %collective-permute-start) | collective-permute-done | bytes 131104 | tf_op jit(solution)/shard_map/while/body/eval_jaxpr/ppermute | solution.py:24
  224.4 1.9 collective-permute-start
  226.3 8.3 %collective-permute-done = f32[2,128,128]{2,1,0:T(8,128)S(1)} collective-permute-done((f32[2,128,128]{2,1,0:T(8,128)S(1)}, f32[2,128,128]{2,1,0:T(8,128)S(1)}, u32[]{:S(2)}, u32[]{:S(2)}) %collective-permute-start) | collective-permute-done | bytes 131104 | tf_op jit(solution)/shard_map/while/body/eval_jaxpr/ppermute | solution.py:24
  234.9 1.9 collective-permute-start
  236.8 7.6 %collective-permute-done = f32[2,128,128]{2,1,0:T(8,128)S(1)} collective-permute-done((f32[2,128,128]{2,1,0:T(8,128)S(1)}, f32[2,128,128]{2,1,0:T(8,128)S(1)}, u32[]{:S(2)}, u32[]{:S(2)}) %collective-permute-start) | collective-permute-done | bytes 131104 | tf_op jit(solution)/shard_map/while/body/eval_jaxpr/ppermute | solution.py:24
  246.6 7.0 %collective-permute-done = f32[2,128,128]{2,1,0:T(8,128)S(1)} collective-permute-done((f32[2,128,128]{2,1,0:T(8,128)S(1)}, f32[2,128,128]{2,1,0:T(8,128)S(1)}, u32[]{:S(2)}, u32[]{:S(2)}) %collective-permute-start) | collective-permute-done | bytes 131104 | tf_op jit(solution)/shard_map/while/body/eval_jaxpr/ppermute | solution.py:24
  254.0 1.9 collective-permute-start
  255.9 7.0 %collective-permute-done = f32[2,128,128]{2,1,0:T(8,128)S(1)} collective-permute-done((f32[2,128,128]{2,1,0:T(8,128)S(1)}, f32[2,128,128]{2,1,0:T(8,128)S(1)}, u32[]{:S(2)}, u32[]{:S(2)}) %collective-permute-start) | collective-permute-done | bytes 131104 | tf_op jit(solution)/shard_map/while/body/eval_jaxpr/ppermute | solution.py:24
  265.1 7.0 %collective-permute-done = f32[2,128,128]{2,1,0:T(8,128)S(1)} collective-permute-done((f32[2,128,128]{2,1,0:T(8,128)S(1)}, f32[2,128,128]{2,1,0:T(8,128)S(1)}, u32[]{:S(2)}, u32[]{:S(2)}) %collective-permute-start) | collective-permute-done | bytes 131104 | tf_op jit(solution)/shard_map/while/body/eval_jaxpr/ppermute | solution.py:24
  274.4 7.0 %collective-permute-done = f32[2,128,128]{2,1,0:T(8,128)S(1)} collective-permute-done((f32[2,128,128]{2,1,0:T(8,128)S(1)}, f32[2,128,128]{2,1,0:T(8,128)S(1)}, u32[]{:S(2)}, u32[]{:S(2)}) %collective-permute-start) | collective-permute-done | bytes 131104 | tf_op jit(solution)/shard_map/while/body/eval_jaxpr/ppermute | solution.py:24
  283.6 7.0 %collective-permute-done = f32[2,128,128]{2,1,0:T(8,128)S(1)} collective-permute-done((f32[2,128,128]{2,1,0:T(8,128)S(1)}, f32[2,128,128]{2,1,0:T(8,128)S(1)}, u32[]{:S(2)}, u32[]{:S(2)}) %collective-permute-start) | collective-permute-done | bytes 131104 | tf_op jit(solution)/shard_map/while/body/eval_jaxpr/ppermute | solution.py:24
  292.9 7.0 %collective-permute-done = f32[2,128,128]{2,1,0:T(8,128)S(1)} collective-permute-done((f32[2,128,128]{2,1,0:T(8,128)S(1)}, f32[2,128,128]{2,1,0:T(8,128)S(1)}, u32[]{:S(2)}, u32[]{:S(2)}) %collective-permute-start) | collective-permute-done | bytes 131104 | tf_op jit(solution)/shard_map/while/body/eval_jaxpr/ppermute | solution.py:24
  299.9 72.7 %while.36 = (s32[]{:T(128)}, f32[2,128,128]{2,1,0:T(8,128)S(1)}, f32[16,2,64,128]{3,2,1,0:T(8,128)S(1)}, f32[16,2]{1,0:T(8,128)S(1)}, f32[16,2,64,128]{3,2,1,0:T...) while((s32[]{:T(128)}, f32[2,128,128]{2,1,0:T(8,128)S(1)}, ...), condition=%wide.region_8.9_spmd, body=%wide.region_7.8_spmd.sunk | while | flops 88178688 | bytes 1248385 | solution.py:127
  (231 shorter events, 166.2 us)
Async XLA Ops:
  0.0 5.0 %copy-start.3 = (bf16[2,1024,128]{2,1,0:T(8,128)(2,1)S(1)}, bf16[2,1024,128]{2,1,0:T(8,128)(2,1)}, u32[]{:S(2)}) copy-start(bf16[2,1024,128]{2,1,0:T(8,128)(2,1)} %param.12) | copy-start | bytes 1572868
  0.0 4.9 %collective-permute-start.1 = (bf16[2,1024,128]{2,1,0:T(8,128)(2,1)}, bf16[2,1024,128]{2,1,0:T(8,128)(2,1)S(1)}, u32[]{:S(2)}, u32[]{:S(2)}) collective-permute-start(bf16[2,1024,128]{2,1,0:T(8,128)(2,1)} %param.12), channel_id=1, source_target_pairs={{0,1},{1,0},{2,3},{3,2},{4,5},{5,4},{6,7},{7,6},{8,9},{9,8},{10,11... | collective-permute-start | bytes 1572872 | tf_op jit(solution)/shard_map/ppermute | solution.py:18
  86.0 1.2 copy-start
  154.2 1.3 copy-start.2
  155.5 144.4 %copy-start.1 = (f32[16,2,64,128]{3,2,1,0:T(8,128)S(1)}, f32[16,2,64,128]{3,2,1,0:T(8,128)}, u32[]{:S(2)}) copy-start(f32[16,2,64,128]{3,2,1,0:T(8,128)} %custom-call.6) | copy-start | bytes 3145732
  158.6 9.9 %collective-permute-start = (f32[2,128,128]{2,1,0:T(8,128)S(1)}, f32[2,128,128]{2,1,0:T(8,128)S(1)}, u32[]{:S(2)}, u32[]{:S(2)}) collective-permute-start(f32[2,128,128]{2,1,0:T(8,128)S(1)} %convolution_add_fusion.7), channel_id=1, source_target_pairs={{0,16},{16,32},{32,48},{48,64},{64,80},{80,96},{96,112},{112,128},... | collective-permute-start | bytes 393224 | tf_op jit(solution)/shard_map/while/body/eval_jaxpr/ppermute | solution.py:24
  168.7 9.0 %collective-permute-start = (f32[2,128,128]{2,1,0:T(8,128)S(1)}, f32[2,128,128]{2,1,0:T(8,128)S(1)}, u32[]{:S(2)}, u32[]{:S(2)}) collective-permute-start(f32[2,128,128]{2,1,0:T(8,128)S(1)} %convolution_add_fusion.7), channel_id=1, source_target_pairs={{0,16},{16,32},{32,48},{48,64},{64,80},{80,96},{96,112},{112,128},... | collective-permute-start | bytes 393224 | tf_op jit(solution)/shard_map/while/body/eval_jaxpr/ppermute | solution.py:24
  178.0 9.0 %collective-permute-start = (f32[2,128,128]{2,1,0:T(8,128)S(1)}, f32[2,128,128]{2,1,0:T(8,128)S(1)}, u32[]{:S(2)}, u32[]{:S(2)}) collective-permute-start(f32[2,128,128]{2,1,0:T(8,128)S(1)} %convolution_add_fusion.7), channel_id=1, source_target_pairs={{0,16},{16,32},{32,48},{48,64},{64,80},{80,96},{96,112},{112,128},... | collective-permute-start | bytes 393224 | tf_op jit(solution)/shard_map/while/body/eval_jaxpr/ppermute | solution.py:24
  187.3 9.0 %collective-permute-start = (f32[2,128,128]{2,1,0:T(8,128)S(1)}, f32[2,128,128]{2,1,0:T(8,128)S(1)}, u32[]{:S(2)}, u32[]{:S(2)}) collective-permute-start(f32[2,128,128]{2,1,0:T(8,128)S(1)} %convolution_add_fusion.7), channel_id=1, source_target_pairs={{0,16},{16,32},{32,48},{48,64},{64,80},{80,96},{96,112},{112,128},... | collective-permute-start | bytes 393224 | tf_op jit(solution)/shard_map/while/body/eval_jaxpr/ppermute | solution.py:24
  196.5 9.0 %collective-permute-start = (f32[2,128,128]{2,1,0:T(8,128)S(1)}, f32[2,128,128]{2,1,0:T(8,128)S(1)}, u32[]{:S(2)}, u32[]{:S(2)}) collective-permute-start(f32[2,128,128]{2,1,0:T(8,128)S(1)} %convolution_add_fusion.7), channel_id=1, source_target_pairs={{0,16},{16,32},{32,48},{48,64},{64,80},{80,96},{96,112},{112,128},... | collective-permute-start | bytes 393224 | tf_op jit(solution)/shard_map/while/body/eval_jaxpr/ppermute | solution.py:24
  205.8 9.0 %collective-permute-start = (f32[2,128,128]{2,1,0:T(8,128)S(1)}, f32[2,128,128]{2,1,0:T(8,128)S(1)}, u32[]{:S(2)}, u32[]{:S(2)}) collective-permute-start(f32[2,128,128]{2,1,0:T(8,128)S(1)} %convolution_add_fusion.7), channel_id=1, source_target_pairs={{0,16},{16,32},{32,48},{48,64},{64,80},{80,96},{96,112},{112,128},... | collective-permute-start | bytes 393224 | tf_op jit(solution)/shard_map/while/body/eval_jaxpr/ppermute | solution.py:24
  215.0 9.1 %collective-permute-start = (f32[2,128,128]{2,1,0:T(8,128)S(1)}, f32[2,128,128]{2,1,0:T(8,128)S(1)}, u32[]{:S(2)}, u32[]{:S(2)}) collective-permute-start(f32[2,128,128]{2,1,0:T(8,128)S(1)} %convolution_add_fusion.7), channel_id=1, source_target_pairs={{0,16},{16,32},{32,48},{48,64},{64,80},{80,96},{96,112},{112,128},... | collective-permute-start | bytes 393224 | tf_op jit(solution)/shard_map/while/body/eval_jaxpr/ppermute | solution.py:24
  224.4 10.2 %collective-permute-start = (f32[2,128,128]{2,1,0:T(8,128)S(1)}, f32[2,128,128]{2,1,0:T(8,128)S(1)}, u32[]{:S(2)}, u32[]{:S(2)}) collective-permute-start(f32[2,128,128]{2,1,0:T(8,128)S(1)} %convolution_add_fusion.7), channel_id=1, source_target_pairs={{0,16},{16,32},{32,48},{48,64},{64,80},{80,96},{96,112},{112,128},... | collective-permute-start | bytes 393224 | tf_op jit(solution)/shard_map/while/body/eval_jaxpr/ppermute | solution.py:24
  234.9 9.5 %collective-permute-start = (f32[2,128,128]{2,1,0:T(8,128)S(1)}, f32[2,128,128]{2,1,0:T(8,128)S(1)}, u32[]{:S(2)}, u32[]{:S(2)}) collective-permute-start(f32[2,128,128]{2,1,0:T(8,128)S(1)} %convolution_add_fusion.7), channel_id=1, source_target_pairs={{0,16},{16,32},{32,48},{48,64},{64,80},{80,96},{96,112},{112,128},... | collective-permute-start | bytes 393224 | tf_op jit(solution)/shard_map/while/body/eval_jaxpr/ppermute | solution.py:24
  244.7 9.0 %collective-permute-start = (f32[2,128,128]{2,1,0:T(8,128)S(1)}, f32[2,128,128]{2,1,0:T(8,128)S(1)}, u32[]{:S(2)}, u32[]{:S(2)}) collective-permute-start(f32[2,128,128]{2,1,0:T(8,128)S(1)} %convolution_add_fusion.7), channel_id=1, source_target_pairs={{0,16},{16,32},{32,48},{48,64},{64,80},{80,96},{96,112},{112,128},... | collective-permute-start | bytes 393224 | tf_op jit(solution)/shard_map/while/body/eval_jaxpr/ppermute | solution.py:24
  254.0 9.0 %collective-permute-start = (f32[2,128,128]{2,1,0:T(8,128)S(1)}, f32[2,128,128]{2,1,0:T(8,128)S(1)}, u32[]{:S(2)}, u32[]{:S(2)}) collective-permute-start(f32[2,128,128]{2,1,0:T(8,128)S(1)} %convolution_add_fusion.7), channel_id=1, source_target_pairs={{0,16},{16,32},{32,48},{48,64},{64,80},{80,96},{96,112},{112,128},... | collective-permute-start | bytes 393224 | tf_op jit(solution)/shard_map/while/body/eval_jaxpr/ppermute | solution.py:24
  263.2 9.0 %collective-permute-start = (f32[2,128,128]{2,1,0:T(8,128)S(1)}, f32[2,128,128]{2,1,0:T(8,128)S(1)}, u32[]{:S(2)}, u32[]{:S(2)}) collective-permute-start(f32[2,128,128]{2,1,0:T(8,128)S(1)} %convolution_add_fusion.7), channel_id=1, source_target_pairs={{0,16},{16,32},{32,48},{48,64},{64,80},{80,96},{96,112},{112,128},... | collective-permute-start | bytes 393224 | tf_op jit(solution)/shard_map/while/body/eval_jaxpr/ppermute | solution.py:24
  272.4 9.0 %collective-permute-start = (f32[2,128,128]{2,1,0:T(8,128)S(1)}, f32[2,128,128]{2,1,0:T(8,128)S(1)}, u32[]{:S(2)}, u32[]{:S(2)}) collective-permute-start(f32[2,128,128]{2,1,0:T(8,128)S(1)} %convolution_add_fusion.7), channel_id=1, source_target_pairs={{0,16},{16,32},{32,48},{48,64},{64,80},{80,96},{96,112},{112,128},... | collective-permute-start | bytes 393224 | tf_op jit(solution)/shard_map/while/body/eval_jaxpr/ppermute | solution.py:24
  281.7 9.0 %collective-permute-start = (f32[2,128,128]{2,1,0:T(8,128)S(1)}, f32[2,128,128]{2,1,0:T(8,128)S(1)}, u32[]{:S(2)}, u32[]{:S(2)}) collective-permute-start(f32[2,128,128]{2,1,0:T(8,128)S(1)} %convolution_add_fusion.7), channel_id=1, source_target_pairs={{0,16},{16,32},{32,48},{48,64},{64,80},{80,96},{96,112},{112,128},... | collective-permute-start | bytes 393224 | tf_op jit(solution)/shard_map/while/body/eval_jaxpr/ppermute | solution.py:24
  290.9 9.0 %collective-permute-start = (f32[2,128,128]{2,1,0:T(8,128)S(1)}, f32[2,128,128]{2,1,0:T(8,128)S(1)}, u32[]{:S(2)}, u32[]{:S(2)}) collective-permute-start(f32[2,128,128]{2,1,0:T(8,128)S(1)} %convolution_add_fusion.7), channel_id=1, source_target_pairs={{0,16},{16,32},{32,48},{48,64},{64,80},{80,96},{96,112},{112,128},... | collective-permute-start | bytes 393224 | tf_op jit(solution)/shard_map/while/body/eval_jaxpr/ppermute | solution.py:24
  372.7 1.0 copy-start.4
  372.7 1.0 copy-start.5
where the time goes:
time: 381 us; the launch traced here: 375 us
  matrix products  143 us (38%)
  waiting for transfers between devices  107 us (28%)
  other arithmetic  82.2 us (22%)
  starting transfers between devices  30.3 us (8%)
  local copies, waits for them, and re-layouts  9.98 us (3%)
    dot_general x145, matrix products, mult(): return jnp.einsum(form, left, right, precision=lax.Precision.HIGHEST)  141 us
    ppermute x15, waiting for transfers between devices, from_behind(): return lax.ppermute(block, axis, route)  107 us
    another operation x4, other arithmetic, solve_lower(): solved = jax.vmap(solver)(flat_sys, flat_rhs)  73 us
    ppermute x15, starting transfers between devices, from_behind(): return lax.ppermute(block, axis, route)  30.3 us
  transfers between devices with their start and end apart: 16, of which 15 were waited for; matrix products, arithmetic and copies ran while one was open for 1% of the time, Pallas kernels for 0%

commit v1 on v0

v1 whole, which is shorter than its diff:
```python
import jax
import jax.numpy as jnp
from jax import lax
from jax.experimental import pallas as pl
from jax.experimental.pallas import tpu as pltpu
from jax.sharding import PartitionSpec as P

MESH = pl.DeviceIdType.MESH
C = 128
D = 128
X = 4
F32 = jnp.float32
BF16 = jnp.bfloat16


def split(a):
    hi = a.astype(BF16)
    return hi, (a - hi.astype(F32)).astype(BF16)


def mm(a, b):
    return lax.dot_general(a, b, (((1,), (0,)), ((), ())), preferred_element_type=F32)


def mm_t(a, b):
    return lax.dot_general(a, b, (((1,), (1,)), ((), ())), preferred_element_type=F32)


def dot3(a, b, mul=mm):
    (ah, al), (bh, bl) = a, b
    n = ah.shape[0]
    both = mul(jnp.concatenate([ah, al], axis=0), bh)
    return both[:n] + (both[n:] + mul(ah, bl))


def dot2(a, b):
    ah, al = a
    n = ah.shape[0]
    both = mm(jnp.concatenate([ah, al], axis=0), b)
    return both[:n] + both[n:]


def iota(shape, dim):
    return lax.broadcasted_iota(jnp.int32, shape, dim)


def inverse(low):
    lanes8 = iota((8, C), 1)
    rows8 = iota((8, C), 0)
    rows = []
    for n in range(C // 8):
        part = low[8 * n : 8 * n + 8]
        inv = jnp.where(lanes8 == rows8 + 8 * n, 1.0, 0.0).astype(F32)
        for j in range(7):
            inv = inv - part[:, 8 * n + j : 8 * n + j + 1] * inv[j : j + 1]
        rows.append(inv)
    b = 8
    while b < C:
        g = b // 8
        pairs = C // (2 * b)
        lane_b = iota((b, C), 1)
        off, odd = [], []
        for p in range(pairs):
            r0 = (2 * p + 1) * b
            inside = (lane_b >= 2 * p * b) & (lane_b < r0)
            off.append(jnp.where(inside, low[r0 : r0 + b], 0.0))
            odd += rows[(2 * p + 1) * g : (2 * p + 2) * g]
        off = jnp.concatenate(off, axis=0)
        odd = jnp.concatenate(odd, axis=0)
        full = jnp.concatenate(rows, axis=0)
        y = dot3(split(off), split(full))
        zero = jnp.zeros((b, C), F32)
        spread = []
        for p in range(pairs):
            spread += [zero, y[p * b : (p + 1) * b]]
        spread = jnp.concatenate(spread, axis=0)
        odd = odd - dot3(split(odd), split(spread))
        for p in range(pairs):
            for i in range(g):
                at = (p * g + i) * 8
                rows[(2 * p + 1) * g + i] = odd[at : at + 8]
        b *= 2
    return jnp.concatenate(rows, axis=0)


def kernel(
    chunks,
    qk_hbm,
    values_ref,
    gate_ref,
    log_ref,
    write_ref,
    gain_ref,
    out_ref,
    qk,
    cum,
    decay,
    wh,
    wl,
    xh,
    xl,
    qah,
    qal,
    ob,
    agat,
    bown,
    bgat,
    srow,
    snext,
    sout,
    sin,
    local_sem,
    send_sem,
    recv_sem,
):
    seq = lax.axis_index("seq")
    head = lax.axis_index("head")
    col = lax.rem(seq, X)
    row = seq // X
    base = row * X
    rows = X
    right = base + lax.rem(col + 1, X)
    left = base + lax.rem(col + X - 1, X)
    across = base + lax.rem(col + 2, X)
    below = lax.rem(row + 1, rows) * X + col
    above = lax.rem(row + rows - 1, rows) * X + col
    parity = lax.rem(head, 2)
    partner = head + 1 - 2 * parity

    barrier = pltpu.get_barrier_semaphore()
    pl.semaphore_signal(barrier, inc=1, device_id={"head": partner}, device_id_type=MESH)
    for other in (right, left, across, below, above):
        pl.semaphore_signal(barrier, inc=1, device_id={"seq": other}, device_id_type=MESH)
    own = pltpu.make_async_copy(qk_hbm, qk.at[parity], local_sem)
    own.start()

    tri = jnp.where(iota((C, C), 0) <= iota((C, C), 1), 1.0, 0.0).astype(F32)
    for r in range(2):
        cum[r] = lax.dot_general(
            log_ref[r],
            tri,
            (((1,), (0,)), ((), ())),
            precision=lax.Precision.HIGHEST,
            preferred_element_type=F32,
        )

    pl.semaphore_wait(barrier, 6)

    def remote(src, dst, index, target, axis="seq"):
        return pltpu.make_async_remote_copy(
            src_ref=src,
            dst_ref=dst,
            send_sem=send_sem.at[index],
            recv_sem=recv_sem.at[index],
            device_id={axis: target},
            device_id_type=MESH,
        )

    swap = remote(qk_hbm, qk.at[parity], 0, partner, "head")
    swap.start()

    eye = iota((C, C), 0) == iota((C, C), 1)
    causal = iota((C, C), 0) >= iota((C, C), 1)
    strict = iota((C, C), 0) > iota((C, C), 1)
    ident = jnp.where(eye, 1.0, 0.0).astype(F32)
    for r in range(2):
        xh[r, 0] = jnp.concatenate([ident, jnp.zeros((C, D), F32)], axis=1).astype(BF16)
        xl[r, 0] = jnp.zeros((C, 2 * D), BF16)

    own.wait()
    swap.wait()

    def first(r, c):
        span = pl.ds(pl.multiple_of(c * C, C), C)
        k = qk[1, r, span, :]
        v = values_ref[r, span, :]
        cum_row = cum[r, pl.ds(c, 1), :]
        w_row = write_ref[r, pl.ds(c, 1), :]
        gram = mm_t(k, k)
        squares = jnp.sum(jnp.where(eye, gram, 0.0), axis=0, keepdims=True)
        rn_row = lax.rsqrt(squares + 1e-06)
        last = cum_row[:, C - 1 : C]
        tail_row = jnp.exp(last - cum_row) * w_row * rn_row
        packed = jnp.concatenate([cum_row, rn_row, tail_row, jnp.zeros((5, C), F32)], axis=0)
        cols = packed.T
        cum_col, rn_col, tail_col = cols[:, 0:1], cols[:, 1:2], cols[:, 2:3]
        spread = jnp.exp(jnp.where(causal, cum_col - cum_row, -1e30)) * (w_row * rn_row)
        decay[r, c] = spread
        low = jnp.where(strict, spread * gram * rn_col, 0.0)
        inv = inverse(low)
        scaled = inv * (jnp.exp(cum_row) * rn_row)
        mix = jnp.concatenate([dot2(split(scaled), k), dot2(split(inv), v)], axis=1)
        mh, ml = split(mix)
        wh[r, c] = mh
        wl[r, c] = ml
        uh, ul = split(mix * tail_col)
        kt = k.T
        ab = mm(kt, uh) + mm(kt, ul)
        step = ident * jnp.exp(last) - ab[:, :D]
        nxt = dot3(split(step), (xh[r, c], xl[r, c]))
        nxt = nxt + jnp.concatenate([jnp.zeros((D, D), F32), ab[:, D:]], axis=1)
        return nxt

    def first_loop(c, _):
        for r in range(2):
            nxt = first(r, c)
            nh, nl = split(nxt)
            xh[r, c + 1] = nh
            xl[r, c + 1] = nl
        return 0

    lax.fori_loop(0, chunks, first_loop, 0)

    sends = []

    def send(*args):
        copy = remote(*args)
        copy.start()
        sends.append(copy)
        return copy

    for r in range(2):
        full = xh[r, chunks].astype(F32) + xl[r, chunks].astype(F32)
        agat[col, r] = full[:, :D]
        bown[r] = full[:, D:].T
    for r in range(2):
        mine = agat.at[col, r]
        send(mine, mine, 1 + r, right)
        send(mine, mine, 3 + r, left)
    block = D // X
    for o, target in ((1, right), (2, across), (3, left)):
        there = pl.ds(pl.multiple_of(lax.rem(col + o, X) * block, block), block)
        send(bown.at[:, there, :], bgat.at[col], 6 + o, target)
    here = pl.ds(pl.multiple_of(col * block, block), block)
    bgat[col] = bown[:, here, :]

    def second(r, c):
        span = pl.ds(pl.multiple_of(c * C, C), C)
        q = qk[0, r, span, :]
        k = qk[1, r, span, :]
        cum_row = cum[r, pl.ds(c, 1), :]
        packed = jnp.broadcast_to(jnp.exp(cum_row), (8, C))
        grow = packed.T[:, 0:1]
        mixing = decay[r, c] * mm_t(q, k)
        both = dot3(split(mixing), (wh[r, c], wl[r, c]))
        lead = grow * q.astype(F32) - both[:, :D]
        res = dot3(split(lead), (xh[r, c], xl[r, c]))
        ah, al = split(res[:, :D])
        qah[r, span, :] = ah
        qal[r, span, :] = al
        ob[r, span, :] = both[:, D:] + res[:, D:]

    def second_loop(c, _):
        for r in range(2):
            second(r, c)
        return 0

    half = chunks // 2
    lax.fori_loop(0, half, second_loop, 0)

    before = lax.rem(col + X - 1, X)
    after = lax.rem(col + 1, X)
    far = lax.rem(col + 2, X)

    def arrival(ref, index):
        return pltpu.make_async_remote_copy(
            src_ref=ref,
            dst_ref=ref,
            send_sem=send_sem.at[index],
            recv_sem=recv_sem.at[index],
            device_id={"seq": right},
            device_id_type=MESH,
        )

    arrival(agat.at[before, 0], 1).wait_recv()
    send(agat.at[before, 0], agat.at[before, 0], 5, right)
    arrival(agat.at[after, 1], 4).wait_recv()
    send(agat.at[after, 1], agat.at[after, 1], 6, left)

    lax.fori_loop(half, chunks, second_loop, 0)

    arrival(agat.at[before, 1], 2).wait_recv()
    arrival(agat.at[after, 0], 3).wait_recv()
    for o in (1, 2, 3):
        arrival(bgat.at[lax.rem(col + X - o, X)], 6 + o).wait_recv()
    arrival(agat.at[far, 0], 5).wait_recv()
    arrival(agat.at[far, 1], 6).wait_recv()

    gains = []
    for r in range(2):
        steps = [split(agat[i, r]) for i in range(X)]
        lead = [None, steps[0]]
        offset = [jnp.zeros((block, D), F32), bgat[0, r]]
        for i in range(1, X):
            lead.append(split(dot3(steps[i], lead[i])))
            offset.append(dot3(split(offset[i]), steps[i], mm_t) + bgat[i, r])
        gains.append((lead, offset))

    @pl.when(row == 0)
    def _():
        srow[...] = jnp.zeros_like(srow)

    @pl.when(row > 0)
    def _():
        arrival(srow, 10).wait_recv()

    state = [split(srow[r]) for r in range(2)]
    for r in range(2):
        lead, offset = gains[r]
        snext[r] = dot3(state[r], lead[X], mm_t) + offset[X]
    down = remote(snext, srow, 10, below)

    @pl.when(row < rows - 1)
    def _():
        down.start()

    for r in range(2):
        lead, offset = gains[r]
        sout[0, r] = srow[r]
        for i in range(1, X):
            sout[i, r] = dot3(state[r], lead[i], mm_t) + offset[i]
    for o, target in ((1, right), (2, across), (3, left)):
        send(sout.at[lax.rem(col + o, X)], sin.at[:, here, :], 10 + o, target)
    sin[:, here, :] = sout[col]
    for o in (1, 2, 3):
        there = pl.ds(pl.multiple_of(lax.rem(col + X - o, X) * block, block), block)
        arrival(sin.at[:, there, :], 10 + o).wait_recv()

    gain = gain_ref[...]

    for r in range(2):
        state_in = split(sin[r])

        def last_loop(c, _):
            span = pl.ds(pl.multiple_of(c * C, C), C)
            raw = ob[r, span, :] + dot3((qah[r, span, :], qal[r, span, :]), state_in, mm_t)
            qf = qk[0, r, span, :].astype(F32)
            raw = raw * lax.rsqrt(jnp.sum(qf * qf, axis=1, keepdims=True) + 1e-06)
            mean = jnp.sum(raw * raw, axis=1, keepdims=True) * (1.0 / D)
            g = gate_ref[r, span, :].astype(F32)
            silu = g / (1.0 + jnp.exp(-g))
            out_ref[r, span, :] = (raw * lax.rsqrt(mean + 1e-06) * gain * silu).astype(BF16)
            return 0

        lax.fori_loop(0, chunks, last_loop, 0)

    for copy in sends:
        copy.wait_send()

    @pl.when(row < rows - 1)
    def _():
        down.wait_send()


def body(query_key, values, out_gate, log_gate, strength, norm_gain):
    requests, length, _ = values.shape
    chunks = length // C
    vmem = pl.BlockSpec(memory_space=pltpu.VMEM)
    wide = (requests, chunks, C, 2 * D)
    block = D // X

    def call(*args):
        return pl.pallas_call(
            lambda *refs: kernel(chunks, *refs),
            out_shape=jax.ShapeDtypeStruct(values.shape, BF16),
            in_specs=[pl.BlockSpec(memory_space=pl.ANY)] + [vmem] * 5,
            out_specs=vmem,
            scratch_shapes=[
                pltpu.VMEM((2,) + query_key.shape, BF16),
                pltpu.VMEM((requests, chunks, C), F32),
                pltpu.VMEM((requests, chunks, C, C), F32),
                pltpu.VMEM(wide, BF16),
                pltpu.VMEM(wide, BF16),
                pltpu.VMEM((requests, chunks + 1, D, 2 * D), BF16),
                pltpu.VMEM((requests, chunks + 1, D, 2 * D), BF16),
                pltpu.VMEM((requests, length, D), BF16),
                pltpu.VMEM((requests, length, D), BF16),
                pltpu.VMEM((requests, length, D), F32),
                pltpu.VMEM((X, requests, D, D), F32),
                pltpu.VMEM((requests, D, D), F32),
                pltpu.VMEM((X, requests, block, D), F32),
                pltpu.VMEM((requests, block, D), F32),
                pltpu.VMEM((requests, block, D), F32),
                pltpu.VMEM((X, requests, block, D), F32),
                pltpu.VMEM((requests, D, D), F32),
                pltpu.SemaphoreType.DMA,
                pltpu.SemaphoreType.DMA((14,)),
                pltpu.SemaphoreType.DMA((14,)),
            ],
            compiler_params=pltpu.CompilerParams(collective_id=0, has_side_effects=True),
        )(*args)

    return call(
        query_key,
        values,
        out_gate,
        log_gate.reshape(requests, chunks, C),
        strength.reshape(requests, chunks, C),
        norm_gain.reshape(1, D),
    )


def solution(mesh):
    return jax.shard_map(
        body,
        mesh=mesh,
        in_specs=(
            P(None, "seq", "head"),
            P(None, "seq", "head"),
            P(None, "seq", "head"),
            P(None, "head", "seq"),
            P(None, "head", "seq"),
            P(),
        ),
        out_specs=P(None, "seq", "head"),
        check_vma=False,
    )
```

time: 381 us -> 71.7 us (0.19); the launches traced: 375 us -> 71.5 us
  matrix products: 143 us -> 0 us
  waiting for transfers between devices: 107 us -> 0 us
  other arithmetic: 82.2 us -> 0 us
  Pallas kernels: 0 us -> 69.6 us
  starting transfers between devices: 30.3 us -> 0 us
  local copies, waits for them, and re-layouts: 9.98 us -> 1.87 us
    dot_general x145 -> x0, matrix products: 141 us -> none  [mult(): return jnp.einsum(form, left, right, precision=lax.Precision.HIGHEST)]
    ppermute x16 -> x0, waiting for transfers between devices: 107 us -> none  [the longest x15 107 us: from_behind(): return lax.ppermute(block, axis, route)]
    another operation x5 -> x0, other arithmetic: 73.4 us -> none  [the longest x4 73 us: solve_lower(): solved = jax.vmap(solver)(flat_sys, flat_rhs)]
    pallas_call x0 -> x1, Pallas kernels: none -> 69.6 us  [call(): pl.pallas_call(lambda *refs: kernel(chunks, *refs), out_shape=jax.ShapeDt...]
    ppermute x16 -> x0, starting transfers between devices: 30.3 us -> none  [the longest x15 30.3 us: from_behind(): return lax.ppermute(block, axis, route)]
  transfers between devices with their start and end apart: 16 -> 0, of which waited for: 15 -> 0; matrix products, arithmetic and copies ran while one was open for 1% -> 0% of each run, Pallas kernels for 0% -> 0%
where the time goes in v1:
time: 71.7 us; the launch traced here: 71.5 us
  Pallas kernels  69.6 us (97%)
  local copies, waits for them, and re-layouts  1.87 us (3%)
    pallas_call x1, Pallas kernels, call(): pl.pallas_call(lambda *refs: kernel(chunks, *refs), out_shape=jax.ShapeDt...  69.6 us
    unnamed x1, local copies, waits for them, and re-layouts  1.87 us

profile of v1, /device:TPU:56, one launch (start us, length us, event | category | flops | bytes accessed | tf_op | source)
XLA Modules:
  0.0 71.5 jit_solution(11397921292981064957)
XLA Ops:
  0.0 69.6 %shard_map.64 = bf16[2,1024,128]{2,1,0:T(8,128)(2,1)} custom-call(bf16[2,1024,128]{2,1,0:T(8,128)(2,1)} %refs_0_.1, bf16[2,1024,128]{2,1,0:T(8,128)(2,1)} %refs_1_.1, bf16[2,1024,128]{2,1,0:T(8,128)(2,1)} %refs_2_.1, f32[2,8,128]{2,1,0:T(8,128)} %bitcast.3, f32[2,8,128]{2,1,0:T(8,128)} %bitcast.4, f32[1,128]{1,0:T(1,128)} %bitcast.5), custom_call_target="tpu_custom_call" | custom-call | tf_op jit(solution)/shard_map/pallas_call | solution.py:363
  69.6 1.9 %copy.8 = bf16[2,1024,128]{2,1,0:T(8,128)(2,1)} copy(bf16[2,1024,128]{2,1,0:T(8,128)(2,1)} %shard_map.64) | data formatting | bytes 1048576

commit v2 on v1

--- a/solution.py
+++ b/solution.py
@@ -9,6 +9,7 @@
 C = 128
 D = 128
 X = 4
+GROUP = 2
 F32 = jnp.float32
 BF16 = jnp.bfloat16
 
@@ -44,43 +45,55 @@
     return lax.broadcasted_iota(jnp.int32, shape, dim)
 
 
-def inverse(low):
+def inverse(lows):
     lanes8 = iota((8, C), 1)
     rows8 = iota((8, C), 0)
-    rows = []
-    for n in range(C // 8):
-        part = low[8 * n : 8 * n + 8]
-        inv = jnp.where(lanes8 == rows8 + 8 * n, 1.0, 0.0).astype(F32)
-        for j in range(7):
-            inv = inv - part[:, 8 * n + j : 8 * n + j + 1] * inv[j : j + 1]
-        rows.append(inv)
+    group8 = lanes8 // 8
+    count = range(len(lows))
+    packs = []
+    for m in count:
+        parts = [jnp.where(group8 == n, lows[m][8 * n : 8 * n + 8], 0.0) for n in range(C // 8)]
+        while len(parts) > 1:
+            parts = [parts[i] + parts[i + 1] for i in range(0, len(parts), 2)]
+        packs.append(parts[0])
+    small = [jnp.where(lanes8 - 8 * group8 == rows8, 1.0, 0.0).astype(F32)] * len(lows)
+    for j in range(7):
+        spot = 8 * group8 + j
+        heads = [jnp.take_along_axis(packs[m], spot, axis=1, mode="promise_in_bounds") for m in count]
+        small = [small[m] - heads[m] * small[m][j : j + 1] for m in count]
+    rows = [[jnp.where(group8 == n, small[m], 0.0) for n in range(C // 8)] for m in count]
     b = 8
     while b < C:
         g = b // 8
         pairs = C // (2 * b)
         lane_b = iota((b, C), 1)
-        off, odd = [], []
-        for p in range(pairs):
-            r0 = (2 * p + 1) * b
-            inside = (lane_b >= 2 * p * b) & (lane_b < r0)
-            off.append(jnp.where(inside, low[r0 : r0 + b], 0.0))
-            odd += rows[(2 * p + 1) * g : (2 * p + 2) * g]
-        off = jnp.concatenate(off, axis=0)
-        odd = jnp.concatenate(odd, axis=0)
-        full = jnp.concatenate(rows, axis=0)
-        y = dot3(split(off), split(full))
         zero = jnp.zeros((b, C), F32)
-        spread = []
-        for p in range(pairs):
-            spread += [zero, y[p * b : (p + 1) * b]]
-        spread = jnp.concatenate(spread, axis=0)
-        odd = odd - dot3(split(odd), split(spread))
-        for p in range(pairs):
-            for i in range(g):
-                at = (p * g + i) * 8
-                rows[(2 * p + 1) * g + i] = odd[at : at + 8]
+        offs, odds, fulls = [], [], []
+        for m in count:
+            off, odd = [], []
+            for p in range(pairs):
+                r0 = (2 * p + 1) * b
+                inside = (lane_b >= 2 * p * b) & (lane_b < r0)
+                off.append(jnp.where(inside, lows[m][r0 : r0 + b], 0.0))
+                odd += rows[m][(2 * p + 1) * g : (2 * p + 2) * g]
+            offs.append(split(jnp.concatenate(off, axis=0)))
+            odds.append(jnp.concatenate(odd, axis=0))
+            fulls.append(split(jnp.concatenate(rows[m], axis=0)))
+        ys = [dot3(offs[m], fulls[m]) for m in count]
+        spreads = []
+        for m in count:
+            spread = []
+            for p in range(pairs):
+                spread += [zero, ys[m][p * b : (p + 1) * b]]
+            spreads.append(split(jnp.concatenate(spread, axis=0)))
+        news = [odds[m] - dot3(split(odds[m]), spreads[m]) for m in count]
+        for m in count:
+            for p in range(pairs):
+                for i in range(g):
+                    at = (p * g + i) * 8
+                    rows[m][(2 * p + 1) * g + i] = news[m][at : at + 8]
         b *= 2
-    return jnp.concatenate(rows, axis=0)
+    return [jnp.concatenate(rows[m], axis=0) for m in count]
 
 
 def kernel(
@@ -97,6 +110,9 @@
     decay,
     wh,
     wl,
+    step_h,
+    step_l,
+    add,
     xh,
     xl,
     qah,
@@ -170,46 +186,72 @@
     own.wait()
     swap.wait()
 
-    def first(r, c):
-        span = pl.ds(pl.multiple_of(c * C, C), C)
-        k = qk[1, r, span, :]
-        v = values_ref[r, span, :]
-        cum_row = cum[r, pl.ds(c, 1), :]
-        w_row = write_ref[r, pl.ds(c, 1), :]
-        gram = mm_t(k, k)
-        squares = jnp.sum(jnp.where(eye, gram, 0.0), axis=0, keepdims=True)
-        rn_row = lax.rsqrt(squares + 1e-06)
-        last = cum_row[:, C - 1 : C]
-        tail_row = jnp.exp(last - cum_row) * w_row * rn_row
-        packed = jnp.concatenate([cum_row, rn_row, tail_row, jnp.zeros((5, C), F32)], axis=0)
-        cols = packed.T
-        cum_col, rn_col, tail_col = cols[:, 0:1], cols[:, 1:2], cols[:, 2:3]
-        spread = jnp.exp(jnp.where(causal, cum_col - cum_row, -1e30)) * (w_row * rn_row)
-        decay[r, c] = spread
-        low = jnp.where(strict, spread * gram * rn_col, 0.0)
-        inv = inverse(low)
-        scaled = inv * (jnp.exp(cum_row) * rn_row)
-        mix = jnp.concatenate([dot2(split(scaled), k), dot2(split(inv), v)], axis=1)
-        mh, ml = split(mix)
-        wh[r, c] = mh
-        wl[r, c] = ml
-        uh, ul = split(mix * tail_col)
-        kt = k.T
-        ab = mm(kt, uh) + mm(kt, ul)
-        step = ident * jnp.exp(last) - ab[:, :D]
-        nxt = dot3(split(step), (xh[r, c], xl[r, c]))
-        nxt = nxt + jnp.concatenate([jnp.zeros((D, D), F32), ab[:, D:]], axis=1)
-        return nxt
-
-    def first_loop(c, _):
+    def first(batch):
+        count = range(len(batch))
+        ks, lows, cum_rows, rn_rows, tails, lasts = [], [], [], [], [], []
+        for r, c in batch:
+            k = qk[1, r, pl.ds(pl.multiple_of(c * C, C), C), :]
+            ks.append(k)
+        grams = [mm_t(k, k) for k in ks]
+        for m in count:
+            r, c = batch[m]
+            cum_row = cum[r, pl.ds(c, 1), :]
+            w_row = write_ref[r, pl.ds(c, 1), :]
+            gram = grams[m]
+            squares = jnp.sum(jnp.where(eye, gram, 0.0), axis=0, keepdims=True)
+            rn_row = lax.rsqrt(squares + 1e-06)
+            last = cum_row[:, C - 1 : C]
+            tail_row = jnp.exp(last - cum_row) * w_row * rn_row
+            packed = jnp.concatenate([cum_row, rn_row, tail_row, jnp.zeros((5, C), F32)], axis=0)
+            cols = packed.T
+            spread = jnp.exp(jnp.where(causal, cols[:, 0:1] - cum_row, -1e30)) * (w_row * rn_row)
+            decay[r, c] = spread
+            lows.append(jnp.where(strict, spread * gram * cols[:, 1:2], 0.0))
+            cum_rows.append(cum_row)
+            rn_rows.append(rn_row)
+            tails.append(cols[:, 2:3])
+            lasts.append(last)
+        invs = inverse(lows)
+        scaleds = [split(invs[m] * (jnp.exp(cum_rows[m]) * rn_rows[m])) for m in count]
+        invs = [split(invs[m]) for m in count]
+        mixes = []
+        for m in count:
+            r, c = batch[m]
+            v = values_ref[r, pl.ds(pl.multiple_of(c * C, C), C), :]
+            mixes.append(jnp.concatenate([dot2(scaleds[m], ks[m]), dot2(invs[m], v)], axis=1))
+        for m in count:
+            r, c = batch[m]
+            mh, ml = split(mixes[m])
+            wh[r, c] = mh
+            wl[r, c] = ml
+            uh, ul = split(mixes[m] * tails[m])
+            kt = ks[m].T
+            ab = mm(kt, uh) + mm(kt, ul)
+            sh, sl = split(ident * jnp.exp(lasts[m]) - ab[:, :D])
+            step_h[r, c] = sh
+            step_l[r, c] = sl
+            add[r, c] = ab[:, D:]
+
+    def scan(r, c):
+        nxt = dot3((step_h[r, c], step_l[r, c]), (xh[r, c], xl[r, c]))
+        nxt = nxt + jnp.concatenate([jnp.zeros((D, D), F32), add[r, c]], axis=1)
+        nh, nl = split(nxt)
+        xh[r, c + 1] = nh
+        xl[r, c + 1] = nl
+
+    first([(r, c) for c in range(GROUP) for r in range(2)])
+
+    def first_loop(i, _):
+        for j in range(GROUP):
+            for r in range(2):
+                scan(r, (i - 1) * GROUP + j)
+        first([(r, i * GROUP + c) for c in range(GROUP) for r in range(2)])
+        return 0
+
+    lax.fori_loop(1, chunks // GROUP, first_loop, 0)
+    for j in range(GROUP):
         for r in range(2):
-            nxt = first(r, c)
-            nh, nl = split(nxt)
-            xh[r, c + 1] = nh
-            xl[r, c + 1] = nl
-        return 0
-
-    lax.fori_loop(0, chunks, first_loop, 0)
+            scan(r, chunks - GROUP + j)
 
     sends = []
 
@@ -234,28 +276,31 @@
     here = pl.ds(pl.multiple_of(col * block, block), block)
     bgat[col] = bown[:, here, :]
 
-    def second(r, c):
-        span = pl.ds(pl.multiple_of(c * C, C), C)
-        q = qk[0, r, span, :]
-        k = qk[1, r, span, :]
-        cum_row = cum[r, pl.ds(c, 1), :]
-        packed = jnp.broadcast_to(jnp.exp(cum_row), (8, C))
-        grow = packed.T[:, 0:1]
-        mixing = decay[r, c] * mm_t(q, k)
-        both = dot3(split(mixing), (wh[r, c], wl[r, c]))
-        lead = grow * q.astype(F32) - both[:, :D]
-        res = dot3(split(lead), (xh[r, c], xl[r, c]))
-        ah, al = split(res[:, :D])
-        qah[r, span, :] = ah
-        qal[r, span, :] = al
-        ob[r, span, :] = both[:, D:] + res[:, D:]
-
-    def second_loop(c, _):
-        for r in range(2):
-            second(r, c)
+    def second(batch):
+        count = range(len(batch))
+        spans = [pl.ds(pl.multiple_of(c * C, C), C) for _, c in batch]
+        qs = [qk[0, batch[m][0], spans[m], :] for m in count]
+        prods = [mm_t(qs[m], qk[1, batch[m][0], spans[m], :]) for m in count]
+        grows, boths, leads = [], [], []
+        for r, c in batch:
+            packed = jnp.broadcast_to(jnp.exp(cum[r, pl.ds(c, 1), :]), (8, C))
+            grows.append(packed.T[:, 0:1])
+        mixings = [split(decay[batch[m]] * prods[m]) for m in count]
+        boths = [dot3(mixings[m], (wh[batch[m]], wl[batch[m]])) for m in count]
+        leads = [split(grows[m] * qs[m].astype(F32) - boths[m][:, :D]) for m in count]
+        for m in count:
+            r, c = batch[m]
+            res = dot3(leads[m], (xh[r, c], xl[r, c]))
+            ah, al = split(res[:, :D])
+            qah[r, spans[m], :] = ah
+            qal[r, spans[m], :] = al
+            ob[r, spans[m], :] = boths[m][:, D:] + res[:, D:]
+
+    def second_loop(i, _):
+        second([(r, i * GROUP + j) for j in range(GROUP) for r in range(2)])
         return 0
 
-    half = chunks // 2
+    half = chunks // GROUP // 2
     lax.fori_loop(0, half, second_loop, 0)
 
     before = lax.rem(col + X - 1, X)
@@ -277,7 +322,7 @@
     arrival(agat.at[after, 1], 4).wait_recv()
     send(agat.at[after, 1], agat.at[after, 1], 6, left)
 
-    lax.fori_loop(half, chunks, second_loop, 0)
+    lax.fori_loop(half, chunks // GROUP, second_loop, 0)
 
     arrival(agat.at[before, 1], 2).wait_recv()
     arrival(agat.at[after, 0], 3).wait_recv()
@@ -328,21 +373,24 @@
 
     gain = gain_ref[...]
 
-    for r in range(2):
-        state_in = split(sin[r])
-
-        def last_loop(c, _):
-            span = pl.ds(pl.multiple_of(c * C, C), C)
-            raw = ob[r, span, :] + dot3((qah[r, span, :], qal[r, span, :]), state_in, mm_t)
+    states = [split(sin[r]) for r in range(2)]
+
+    def last_loop(c, _):
+        span = pl.ds(pl.multiple_of(c * C, C), C)
+        raws = [
+            ob[r, span, :] + dot3((qah[r, span, :], qal[r, span, :]), states[r], mm_t)
+            for r in range(2)
+        ]
+        for r in range(2):
             qf = qk[0, r, span, :].astype(F32)
-            raw = raw * lax.rsqrt(jnp.sum(qf * qf, axis=1, keepdims=True) + 1e-06)
+            raw = raws[r] * lax.rsqrt(jnp.sum(qf * qf, axis=1, keepdims=True) + 1e-06)
             mean = jnp.sum(raw * raw, axis=1, keepdims=True) * (1.0 / D)
             g = gate_ref[r, span, :].astype(F32)
             silu = g / (1.0 + jnp.exp(-g))
             out_ref[r, span, :] = (raw * lax.rsqrt(mean + 1e-06) * gain * silu).astype(BF16)
-            return 0
-
-        lax.fori_loop(0, chunks, last_loop, 0)
+        return 0
+
+    lax.fori_loop(0, chunks, last_loop, 0)
 
     for copy in sends:
         copy.wait_send()
@@ -371,6 +419,9 @@
                 pltpu.VMEM((requests, chunks, C, C), F32),
                 pltpu.VMEM(wide, BF16),
                 pltpu.VMEM(wide, BF16),
+                pltpu.VMEM((requests, chunks, D, D), BF16),
+                pltpu.VMEM((requests, chunks, D, D), BF16),
+                pltpu.VMEM((requests, chunks, D, D), F32),
                 pltpu.VMEM((requests, chunks + 1, D, 2 * D), BF16),
                 pltpu.VMEM((requests, chunks + 1, D, 2 * D), BF16),
                 pltpu.VMEM((requests, length, D), BF16),

time: 71.7 us -> 45.9 us (0.64)
  Pallas kernels: 69.6 us -> 43.9 us
    pallas_call x1, Pallas kernels: 69.6 us -> 43.9 us  [call(): pl.pallas_call(lambda *refs: kernel(chunks, *refs), out_shape=jax.ShapeDt...]
where the time goes in v2:
time: 45.9 us; the launch traced here: 45.8 us
  Pallas kernels  43.9 us (96%)
  local copies, waits for them, and re-layouts  1.87 us (4%)
    pallas_call x1, Pallas kernels, call(): pl.pallas_call(lambda *refs: kernel(chunks, *refs), out_shape=jax.ShapeDt...  43.9 us
    unnamed x1, local copies, waits for them, and re-layouts  1.87 us

profile of v2, /device:TPU:56, one launch (start us, length us, event | category | flops | bytes accessed | tf_op | source)
XLA Modules:
  0.0 45.8 jit_solution(9221071046216884833)
XLA Ops:
  0.0 43.9 %shard_map.64 = bf16[2,1024,128]{2,1,0:T(8,128)(2,1)} custom-call(bf16[2,1024,128]{2,1,0:T(8,128)(2,1)} %refs_0_.1, bf16[2,1024,128]{2,1,0:T(8,128)(2,1)} %refs_1_.1, bf16[2,1024,128]{2,1,0:T(8,128)(2,1)} %refs_2_.1, f32[2,8,128]{2,1,0:T(8,128)} %bitcast.3, f32[2,8,128]{2,1,0:T(8,128)} %bitcast.4, f32[1,128]{1,0:T(1,128)} %bitcast.5), custom_call_target="tpu_custom_call" | custom-call | tf_op jit(solution)/shard_map/pallas_call | solution.py:411
  43.9 1.9 %copy.8 = bf16[2,1024,128]{2,1,0:T(8,128)(2,1)} copy(bf16[2,1024,128]{2,1,0:T(8,128)(2,1)} %shard_map.64) | data formatting | bytes 1048576

commit v3 on v2

v3 whole, which is shorter than its diff:
```python
import jax
import jax.numpy as jnp
from jax import lax
from jax.experimental import pallas as pl
from jax.experimental.pallas import tpu as pltpu
from jax.sharding import PartitionSpec as P

MESH = pl.DeviceIdType.MESH
C = 128
D = 128
X = 4
GROUP = 4
GROUPS = 2
F32 = jnp.float32
BF16 = jnp.bfloat16


def split(a):
    hi = a.astype(BF16)
    return hi, (a - hi.astype(F32)).astype(BF16)


def mm(a, b):
    return lax.dot_general(a, b, (((1,), (0,)), ((), ())), preferred_element_type=F32)


def mm_t(a, b):
    return lax.dot_general(a, b, (((1,), (1,)), ((), ())), preferred_element_type=F32)


def dot3(a, b, mul=mm):
    (ah, al), (bh, bl) = a, b
    n = ah.shape[0]
    both = mul(jnp.concatenate([ah, al], axis=0), bh)
    return both[:n] + (both[n:] + mul(ah, bl))


def dot2(a, b):
    ah, al = a
    n = ah.shape[0]
    both = mm(jnp.concatenate([ah, al], axis=0), b)
    return both[:n] + both[n:]


def iota(shape, dim):
    return lax.broadcasted_iota(jnp.int32, shape, dim)


def inverse(lows):
    lanes8 = iota((8, C), 1)
    rows8 = iota((8, C), 0)
    group8 = lanes8 // 8
    count = range(len(lows))
    packs = []
    for m in count:
        parts = [jnp.where(group8 == n, lows[m][8 * n : 8 * n + 8], 0.0) for n in range(C // 8)]
        while len(parts) > 1:
            parts = [parts[i] + parts[i + 1] for i in range(0, len(parts), 2)]
        packs.append(parts[0])
    small = [jnp.where(lanes8 - 8 * group8 == rows8, 1.0, 0.0).astype(F32)] * len(lows)
    for j in range(7):
        spot = 8 * group8 + j
        heads = [jnp.take_along_axis(packs[m], spot, axis=1, mode="promise_in_bounds") for m in count]
        small = [small[m] - heads[m] * small[m][j : j + 1] for m in count]
    rows = [[jnp.where(group8 == n, small[m], 0.0) for n in range(C // 8)] for m in count]
    b = 8
    while b < C:
        g = b // 8
        pairs = C // (2 * b)
        lane_b = iota((b, C), 1)
        zero = jnp.zeros((b, C), F32)
        offs, odds, fulls = [], [], []
        for m in count:
            off, odd = [], []
            for p in range(pairs):
                r0 = (2 * p + 1) * b
                inside = (lane_b >= 2 * p * b) & (lane_b < r0)
                off.append(jnp.where(inside, lows[m][r0 : r0 + b], 0.0))
                odd += rows[m][(2 * p + 1) * g : (2 * p + 2) * g]
            offs.append(split(jnp.concatenate(off, axis=0)))
            odds.append(jnp.concatenate(odd, axis=0))
            fulls.append(split(jnp.concatenate(rows[m], axis=0)))
        ys = [dot3(offs[m], fulls[m]) for m in count]
        spreads = []
        for m in count:
            spread = []
            for p in range(pairs):
                spread += [zero, ys[m][p * b : (p + 1) * b]]
            spreads.append(split(jnp.concatenate(spread, axis=0)))
        news = [odds[m] - dot3(split(odds[m]), spreads[m]) for m in count]
        for m in count:
            for p in range(pairs):
                for i in range(g):
                    at = (p * g + i) * 8
                    rows[m][(2 * p + 1) * g + i] = news[m][at : at + 8]
        b *= 2
    return [jnp.concatenate(rows[m], axis=0) for m in count]


def semaphores():
    names = [("swap", i) for i in range(2 * GROUPS)]
    for r in range(2):
        names += [(kind, r) for kind in ("right", "left", "far_right", "far_left")]
        names += [(kind, o, r) for kind in ("block", "state") for o in (1, 2, 3)]
        names += [("offset", s, d, r) for s in range(X) for d in range(s + 1, X)]
        names += [("gain", s, d, r) for s in range(1, X) for d in range(s + 1, X)]
    return {name: i for i, name in enumerate(names)}


SEM = semaphores()


def kernel(
    chunks,
    qk_hbm,
    values_hbm,
    gate_hbm,
    log_ref,
    write_ref,
    gain_ref,
    out_hbm,
    qk,
    values_ref,
    gate_ref,
    out_ref,
    cum,
    decay,
    wh,
    wl,
    step_h,
    step_l,
    add,
    xh,
    xl,
    qah,
    qal,
    ob,
    agat,
    bown,
    bgat,
    lead_h,
    lead_l,
    offs,
    comp,
    inv_h,
    inv_l,
    tails,
    ya,
    yb,
    srow,
    sout,
    sin,
    local_sem,
    send_sem,
    recv_sem,
):
    seq = lax.axis_index("seq")
    head = lax.axis_index("head")
    col = lax.rem(seq, X)
    row = seq // X
    base = row * X
    after = lax.rem(col + 1, X)
    far = lax.rem(col + 2, X)
    before = lax.rem(col + X - 1, X)
    right, across, left = base + after, base + far, base + before
    parity = lax.rem(head, 2)
    partner = head + 1 - 2 * parity

    barrier = pltpu.get_barrier_semaphore()
    pl.semaphore_signal(barrier, inc=1, device_id={"head": partner}, device_id_type=MESH)
    for other in (right, left, across):
        pl.semaphore_signal(barrier, inc=1, device_id={"seq": other}, device_id_type=MESH)
    for o in range(1, X):
        other = lax.rem(row + o, X) * X + col
        pl.semaphore_signal(barrier, inc=1, device_id={"seq": other}, device_id_type=MESH)
    own = pltpu.make_async_copy(qk_hbm, qk.at[parity], local_sem.at[0])
    own.start()
    take_values = pltpu.make_async_copy(values_hbm, values_ref, local_sem.at[1])
    take_values.start()
    take_gate = pltpu.make_async_copy(gate_hbm, gate_ref, local_sem.at[2])
    take_gate.start()

    tri = jnp.where(iota((C, C), 0) <= iota((C, C), 1), 1.0, 0.0).astype(F32)
    for r in range(2):
        cum[r] = lax.dot_general(
            log_ref[r],
            tri,
            (((1,), (0,)), ((), ())),
            precision=lax.Precision.HIGHEST,
            preferred_element_type=F32,
        )

    def remote(src, dst, name, target, axis="seq"):
        return pltpu.make_async_remote_copy(
            src_ref=src,
            dst_ref=dst,
            send_sem=send_sem.at[SEM[name]],
            recv_sem=recv_sem.at[SEM[name]],
            device_id={axis: target},
            device_id_type=MESH,
        )

    sends = []

    def send(*args):
        copy = remote(*args)
        copy.start()
        sends.append(copy)

    def arrive(ref, name):
        remote(ref, ref, name, right).wait_recv()

    pl.semaphore_wait(barrier, 7)
    swaps = []
    for i in range(2 * GROUPS):
        part = pl.ds(i % GROUPS * GROUP * C, GROUP * C)
        src, dst = qk_hbm.at[i // GROUPS, part, :], qk.at[parity, i // GROUPS, part, :]
        swaps.append(remote(src, dst, ("swap", i), partner, "head"))
        swaps[i].start()

    eye = iota((C, C), 0) == iota((C, C), 1)
    causal = iota((C, C), 0) >= iota((C, C), 1)
    strict = iota((C, C), 0) > iota((C, C), 1)
    ident = jnp.where(eye, 1.0, 0.0).astype(F32)
    for r in range(2):
        xh[r, 0] = jnp.concatenate([ident, jnp.zeros((C, D), F32)], axis=1).astype(BF16)
        xl[r, 0] = jnp.zeros((C, 2 * D), BF16)

    own.wait()
    take_values.wait()
    swaps[0].wait_recv()

    def first(batch, full):
        count = range(len(batch))
        ks, lows, cum_rows, rn_rows, tails_col, lasts = [], [], [], [], [], []
        for r, c in batch:
            k = qk[1, r, pl.ds(pl.multiple_of(c * C, C), C), :]
            ks.append(k)
        grams = [mm_t(k, k) for k in ks]
        for m in count:
            r, c = batch[m]
            cum_row = cum[r, pl.ds(c, 1), :]
            w_row = write_ref[r, pl.ds(c, 1), :]
            gram = grams[m]
            squares = jnp.sum(jnp.where(eye, gram, 0.0), axis=0, keepdims=True)
            rn_row = lax.rsqrt(squares + 1e-06)
            last = cum_row[:, C - 1 : C]
            tail_row = jnp.exp(last - cum_row) * w_row * rn_row
            packed = jnp.concatenate([cum_row, rn_row, tail_row, jnp.zeros((5, C), F32)], axis=0)
            cols = packed.T
            spread = jnp.exp(jnp.where(causal, cols[:, 0:1] - cum_row, -1e30)) * (w_row * rn_row)
            decay[r, c] = spread
            lows.append(jnp.where(strict, spread * gram * cols[:, 1:2], 0.0))
            cum_rows.append(cum_row)
            rn_rows.append(rn_row)
            tails_col.append(cols[:, 2:3])
            if not full:
                tails[c : c + 1, :] = tail_row
            lasts.append(last)
        invs = inverse(lows)
        scaleds = [split(invs[m] * (jnp.exp(cum_rows[m]) * rn_rows[m])) for m in count]
        invs = [split(invs[m]) for m in count]
        mixes = [dot2(scaleds[m], ks[m]) for m in count]
        if full:
            for m in count:
                r, c = batch[m]
                v = values_ref[r, pl.ds(pl.multiple_of(c * C, C), C), :]
                mixes[m] = jnp.concatenate([mixes[m], dot2(invs[m], v)], axis=1)
        for m in count:
            r, c = batch[m]
            width = mixes[m].shape[1]
            wh[r, c, :, 0:width], wl[r, c, :, 0:width] = split(mixes[m])
            uh, ul = split(mixes[m] * tails_col[m])
            kt = ks[m].T
            ab = mm(kt, uh) + mm(kt, ul)
            step_h[r, c], step_l[r, c] = split(ident * jnp.exp(lasts[m]) - ab[:, :D])
            if full:
                add[r, c] = ab[:, D:]
            else:
                inv_h[c], inv_l[c] = invs[m]

    def late(cs):
        vs = [values_ref[1, pl.ds(c * C, C), :] for c in cs]
        mixes = [dot2((inv_h[c], inv_l[c]), v) for c, v in zip(cs, vs)]
        for c, mix in zip(cs, mixes):
            col_tail = jnp.broadcast_to(tails[c : c + 1, :], (8, C)).T[:, 0:1]
            wh[1, c, :, D:], wl[1, c, :, D:] = split(mix)
            uh, ul = split(mix * col_tail)
            kt = qk[1, 1, pl.ds(c * C, C), :].T
            add[1, c] = mm(kt, uh) + mm(kt, ul)

    def scan(r, c, lo, hi):
        nxt = dot3((step_h[r, c], step_l[r, c]), (xh[r, c, :, lo:hi], xl[r, c, :, lo:hi]))
        if hi - lo == 2 * D:
            nxt = nxt + jnp.concatenate([jnp.zeros((D, D), F32), add[r, c]], axis=1)
        elif lo == D:
            nxt = nxt + add[r, c]
        xh[r, c + 1, :, lo:hi], xl[r, c + 1, :, lo:hi] = split(nxt)

    def group(g):
        return [(g // GROUPS, g % GROUPS * GROUP + j) for j in range(GROUP)]

    def stage(g):
        for r, c in group(g - 1):
            scan(r, c, 0, D if r else 2 * D)
        first(group(g), g < GROUPS)

    block = D // X
    here = pl.ds(pl.multiple_of(col * block, block), block)

    def section(r, lo):
        hi = lo + D
        return xh[r, chunks, :, lo:hi].astype(F32) + xl[r, chunks, :, lo:hi].astype(F32)

    def send_gain(r):
        agat[col, r] = section(r, 0)
        mine = agat.at[col, r]
        send(mine, mine, ("right", r), right)
        send(mine, mine, ("left", r), left)

    def send_offset(r):
        bown[r] = section(r, D).T
        for o, target in ((1, right), (2, across), (3, left)):
            there = pl.ds(pl.multiple_of(lax.rem(col + o, X) * block, block), block)
            send(bown.at[r, there, :], bgat.at[col, r], ("block", o, r), target)
        bgat[col, r] = bown[r, here, :]

    half = D // 2

    def forward(r):
        arrive(agat.at[before, r], ("right", r))
        part = agat.at[before, r, pl.ds(0, half), :]
        send(part, part, ("far_right", r), right)
        arrive(agat.at[after, r], ("left", r))
        part = agat.at[after, r, pl.ds(half, half), :]
        send(part, part, ("far_left", r), left)

    def compose(r):
        arrive(agat.at[far, r, pl.ds(0, half), :], ("far_right", r))
        arrive(agat.at[far, r, pl.ds(half, half), :], ("far_left", r))
        steps = [split(agat[i, r]) for i in range(X)]
        lead = steps[0]
        lead_h[r, 0], lead_l[r, 0] = lead
        for i in range(1, X):
            whole = dot3(steps[i], lead)
            if i < X - 1:
                lead = split(whole)
                lead_h[r, i], lead_l[r, i] = lead
            else:
                comp[r] = whole
        push(gains, r)
        for o in (1, 2, 3):
            arrive(bgat.at[lax.rem(col + X - o, X), r], ("block", o, r))
        offset = bgat[0, r]
        offs[r, 0] = offset
        for i in range(1, X):
            offset = dot3(split(offset), steps[i], mm_t) + bgat[i, r]
            offs[r, i] = offset
        push(offsets, r)

    def gains(r, s):
        if s == 0:
            return []
        return [
            remote(comp.at[r], ya.at[s - 1, r], ("gain", s, d, r), d * X + col)
            for d in range(s + 1, X)
        ]

    def offsets(r, s):
        return [
            remote(offs.at[r, X - 1], yb.at[s, r], ("offset", s, d, r), d * X + col)
            for d in range(s + 1, X)
        ]

    def push(copies, r):
        for s in range(X - 1):

            @pl.when(row == s)
            def _(s=s):
                for copy in copies(r, s):
                    copy.start()

    def settle(r):
        for d in range(X):

            @pl.when(row == d)
            def _(d=d):
                state = jnp.zeros((block, D), F32)
                for s in range(d):
                    if s == 0:
                        arrive(yb.at[0, r], ("offset", 0, d, r))
                        state = yb[0, r]
                    else:
                        arrive(ya.at[s - 1, r], ("gain", s, d, r))
                        matrix = split(ya[s - 1, r])
                        arrive(yb.at[s, r], ("offset", s, d, r))
                        state = dot3(split(state), matrix, mm_t) + yb[s, r]
                srow[r] = state

        state = split(srow[r])
        sout[0, r] = srow[r]
        for i in range(1, X):
            lead = (lead_h[r, i - 1], lead_l[r, i - 1])
            sout[i, r] = dot3(state, lead, mm_t) + offs[r, i - 1]
        for o, target in ((1, right), (2, across), (3, left)):
            dst = sin.at[r, here, :]
            send(sout.at[lax.rem(col + o, X), r], dst, ("state", o, r), target)
        sin[r, here, :] = sout[col, r]

    first(group(0), True)
    for i in range(1, 2 * GROUPS):
        swaps[i].wait_recv()
    for g in range(1, GROUPS + 1):
        stage(g)
    send_gain(0)
    send_offset(0)
    for g in range(GROUPS + 1, 2 * GROUPS):
        stage(g)
    forward(0)
    for r, c in group(2 * GROUPS - 1):
        scan(r, c, 0, D)
    send_gain(1)
    late(range(GROUP))
    for g in range(1, GROUPS):
        for j in range(GROUP):
            scan(1, (g - 1) * GROUP + j, D, 2 * D)
        late(range(g * GROUP, (g + 1) * GROUP))
    for j in range(GROUP):
        scan(1, chunks - GROUP + j, D, 2 * D)
    send_offset(1)
    forward(1)

    def second(batch):
        count = range(len(batch))
        spans = [pl.ds(pl.multiple_of(c * C, C), C) for _, c in batch]
        qs = [qk[0, batch[m][0], spans[m], :] for m in count]
        prods = [mm_t(qs[m], qk[1, batch[m][0], spans[m], :]) for m in count]
        grows, boths, leads = [], [], []
        for r, c in batch:
            packed = jnp.broadcast_to(jnp.exp(cum[r, pl.ds(c, 1), :]), (8, C))
            grows.append(packed.T[:, 0:1])
        mixings = [split(decay[batch[m]] * prods[m]) for m in count]
        boths = [dot3(mixings[m], (wh[batch[m]], wl[batch[m]])) for m in count]
        leads = [split(grows[m] * qs[m].astype(F32) - boths[m][:, :D]) for m in count]
        for m in count:
            r, c = batch[m]
            res = dot3(leads[m], (xh[r, c], xl[r, c]))
            ah, al = split(res[:, :D])
            qah[r, spans[m], :] = ah
            qal[r, spans[m], :] = al
            ob[r, spans[m], :] = boths[m][:, D:] + res[:, D:]

    compose(0)
    second(group(0))
    compose(1)
    second(group(1))
    settle(0)
    second(group(2))
    second(group(3))
    settle(1)

    gain = gain_ref[...]
    take_gate.wait()
    puts = []
    for r in range(2):
        for o in (1, 2, 3):
            there = pl.ds(pl.multiple_of(lax.rem(col + X - o, X) * block, block), block)
            arrive(sin.at[r, there, :], ("state", o, r))
        state = split(sin[r])

        def last_loop(i, _):
            spans = [pl.ds(pl.multiple_of((2 * i + j) * C, C), C) for j in range(2)]
            raws = [
                ob[r, span, :] + dot3((qah[r, span, :], qal[r, span, :]), state, mm_t)
                for span in spans
            ]
            for j in range(2):
                span = spans[j]
                qf = qk[0, r, span, :].astype(F32)
                raw = raws[j] * lax.rsqrt(jnp.sum(qf * qf, axis=1, keepdims=True) + 1e-06)
                mean = jnp.sum(raw * raw, axis=1, keepdims=True) * (1.0 / D)
                g = gate_ref[r, span, :].astype(F32)
                silu = g / (1.0 + jnp.exp(-g))
                out_ref[r, span, :] = (raw * lax.rsqrt(mean + 1e-06) * gain * silu).astype(BF16)
            return 0

        lax.fori_loop(0, chunks // 2, last_loop, 0)
        put = pltpu.make_async_copy(out_ref.at[r], out_hbm.at[r], local_sem.at[3 + r])
        put.start()
        puts.append(put)

    for copy in swaps:
        copy.wait_send()
    for copy in sends:
        copy.wait_send()
    for s in range(X - 1):

        @pl.when(row == s)
        def _(s=s):
            for r in range(2):
                for copy in gains(r, s) + offsets(r, s):
                    copy.wait_send()

    for put in puts:
        put.wait()


def body(query_key, values, out_gate, log_gate, strength, norm_gain):
    requests, length, _ = values.shape
    chunks = length // C
    vmem = pl.BlockSpec(memory_space=pltpu.VMEM)
    wide = (requests, chunks, C, 2 * D)
    block = D // X

    def call(*args):
        return pl.pallas_call(
            lambda *refs: kernel(chunks, *refs),
            out_shape=jax.ShapeDtypeStruct(values.shape, BF16),
            in_specs=[pl.BlockSpec(memory_space=pl.ANY)] * 3 + [vmem] * 3,
            out_specs=pl.BlockSpec(memory_space=pl.ANY),
            scratch_shapes=[
                pltpu.VMEM((2,) + query_key.shape, BF16),
                pltpu.VMEM(values.shape, BF16),
                pltpu.VMEM(values.shape, BF16),
                pltpu.VMEM(values.shape, BF16),
                pltpu.VMEM((requests, chunks, C), F32),
                pltpu.VMEM((requests, chunks, C, C), F32),
                pltpu.VMEM(wide, BF16),
                pltpu.VMEM(wide, BF16),
                pltpu.VMEM((requests, chunks, D, D), BF16),
                pltpu.VMEM((requests, chunks, D, D), BF16),
                pltpu.VMEM((requests, chunks, D, D), F32),
                pltpu.VMEM((requests, chunks + 1, D, 2 * D), BF16),
                pltpu.VMEM((requests, chunks + 1, D, 2 * D), BF16),
                pltpu.VMEM((requests, length, D), BF16),
                pltpu.VMEM((requests, length, D), BF16),
                pltpu.VMEM((requests, length, D), F32),
                pltpu.VMEM((X, requests, D, D), F32),
                pltpu.VMEM((requests, D, D), F32),
                pltpu.VMEM((X, requests, block, D), F32),
                pltpu.VMEM((requests, X - 1, D, D), BF16),
                pltpu.VMEM((requests, X - 1, D, D), BF16),
                pltpu.VMEM((requests, X, block, D), F32),
                pltpu.VMEM((requests, D, D), F32),
                pltpu.VMEM((chunks, C, C), BF16),
                pltpu.VMEM((chunks, C, C), BF16),
                pltpu.VMEM((chunks, C), F32),
                pltpu.VMEM((X - 2, requests, D, D), F32),
                pltpu.VMEM((X - 1, requests, block, D), F32),
                pltpu.VMEM((requests, block, D), F32),
                pltpu.VMEM((X, requests, block, D), F32),
                pltpu.VMEM((requests, D, D), F32),
                pltpu.SemaphoreType.DMA((5,)),
                pltpu.SemaphoreType.DMA((len(SEM),)),
                pltpu.SemaphoreType.DMA((len(SEM),)),
            ],
            compiler_params=pltpu.CompilerParams(collective_id=0, has_side_effects=True),
        )(*args)

    return call(
        query_key,
        values,
        out_gate,
        log_gate.reshape(requests, chunks, C),
        strength.reshape(requests, chunks, C),
        norm_gain.reshape(1, D),
    )


def solution(mesh):
    return jax.shard_map(
        body,
        mesh=mesh,
        in_specs=(
            P(None, "seq", "head"),
            P(None, "seq", "head"),
            P(None, "seq", "head"),
            P(None, "head", "seq"),
            P(None, "head", "seq"),
            P(),
        ),
        out_specs=P(None, "seq", "head"),
        check_vma=False,
    )
```

time: 45.9 us -> 39.1 us (0.85)
  Pallas kernels: 43.9 us -> 37.1 us
    pallas_call x1, Pallas kernels: 43.9 us -> 37.1 us  [call(): pl.pallas_call(lambda *refs: kernel(chunks, *refs), out_shape=jax.ShapeDt...]
where the time goes in v3:
time: 39.1 us; the launch traced here: 38.9 us
  Pallas kernels  37.1 us (95%)
  local copies, waits for them, and re-layouts  1.87 us (5%)
    pallas_call x1, Pallas kernels, call(): pl.pallas_call(lambda *refs: kernel(chunks, *refs), out_shape=jax.ShapeDt...  37.1 us
    unnamed x1, local copies, waits for them, and re-layouts  1.87 us

profile of v3, /device:TPU:56, one launch (start us, length us, event | category | flops | bytes accessed | tf_op | source)
XLA Modules:
  0.0 38.9 jit_solution(4716979783037490748)
XLA Ops:
  0.0 37.1 %shard_map.64 = bf16[2,1024,128]{2,1,0:T(8,128)(2,1)} custom-call(bf16[2,1024,128]{2,1,0:T(8,128)(2,1)} %refs_0_.1, bf16[2,1024,128]{2,1,0:T(8,128)(2,1)} %refs_1_.1, bf16[2,1024,128]{2,1,0:T(8,128)(2,1)} %refs_2_.1, f32[2,8,128]{2,1,0:T(8,128)} %bitcast.3, f32[2,8,128]{2,1,0:T(8,128)} %bitcast.4, f32[1,128]{1,0:T(1,128)} %bitcast.5), custom_call_target="tpu_custom_call" | custom-call | tf_op jit(solution)/shard_map/pallas_call | solution.py:516
  37.1 1.9 %copy.8 = bf16[2,1024,128]{2,1,0:T(8,128)(2,1)} copy(bf16[2,1024,128]{2,1,0:T(8,128)(2,1)} %shard_map.64) | data formatting | bytes 1048576

commit v4 on v3

--- a/solution.py
+++ b/solution.py
@@ -11,6 +11,7 @@
 X = 4
 GROUP = 4
 GROUPS = 2
+SMALL = 16
 F32 = jnp.float32
 BF16 = jnp.bfloat16
 
@@ -47,23 +48,38 @@
 
 
 def inverse(lows):
-    lanes8 = iota((8, C), 1)
-    rows8 = iota((8, C), 0)
-    group8 = lanes8 // 8
+    lanes = iota((8, C), 1)
+    octet = iota((8, C), 0)
+    patch = lanes // SMALL
+    inside = lanes - SMALL * patch
     count = range(len(lows))
+    levels = SMALL // 8
+    blocks = C // SMALL
     packs = []
     for m in count:
-        parts = [jnp.where(group8 == n, lows[m][8 * n : 8 * n + 8], 0.0) for n in range(C // 8)]
-        while len(parts) > 1:
-            parts = [parts[i] + parts[i + 1] for i in range(0, len(parts), 2)]
-        packs.append(parts[0])
-    small = [jnp.where(lanes8 - 8 * group8 == rows8, 1.0, 0.0).astype(F32)] * len(lows)
-    for j in range(7):
-        spot = 8 * group8 + j
-        heads = [jnp.take_along_axis(packs[m], spot, axis=1, mode="promise_in_bounds") for m in count]
-        small = [small[m] - heads[m] * small[m][j : j + 1] for m in count]
-    rows = [[jnp.where(group8 == n, small[m], 0.0) for n in range(C // 8)] for m in count]
-    b = 8
+        pack = []
+        for q in range(levels):
+            total = None
+            for n in range(blocks):
+                at = SMALL * n + 8 * q
+                part = jnp.where(patch == n, lows[m][at : at + 8], 0.0)
+                total = part if total is None else total + part
+            pack.append(total)
+        packs.append(pack)
+    unit = [jnp.where(inside == octet + 8 * q, 1.0, 0.0).astype(F32) for q in range(levels)]
+    small = [list(unit) for _ in count]
+    for j in range(SMALL - 1):
+        spot = SMALL * patch + j
+        for m in count:
+            pivot = small[m][j // 8][j % 8 : j % 8 + 1]
+            for q in range((j + 1) // 8, levels):
+                head = jnp.take_along_axis(packs[m][q], spot, axis=1, mode="promise_in_bounds")
+                small[m][q] = small[m][q] - head * pivot
+    rows = [
+        [jnp.where(patch == n, small[m][q], 0.0) for n in range(blocks) for q in range(levels)]
+        for m in count
+    ]
+    b = SMALL
     while b < C:
         g = b // 8
         pairs = C // (2 * b)
@@ -100,7 +116,7 @@
 def semaphores():
     names = [("swap", i) for i in range(2 * GROUPS)]
     for r in range(2):
-        names += [(kind, r) for kind in ("right", "left", "far_right", "far_left")]
+        names += [(kind, r) for kind in ("right", "right2", "left", "left2", "far_right", "far_left")]
         names += [(kind, o, r) for kind in ("block", "state") for o in (1, 2, 3)]
         names += [("offset", s, d, r) for s in range(X) for d in range(s + 1, X)]
         names += [("gain", s, d, r) for s in range(1, X) for d in range(s + 1, X)]
@@ -135,6 +151,7 @@
     qah,
     qal,
     ob,
+    amp,
     agat,
     bown,
     bgat,
@@ -314,9 +331,11 @@
 
     def send_gain(r):
         agat[col, r] = section(r, 0)
-        mine = agat.at[col, r]
-        send(mine, mine, ("right", r), right)
-        send(mine, mine, ("left", r), left)
+        top, low = (agat.at[col, r, pl.ds(i * half, half), :] for i in range(2))
+        send(top, top, ("right", r), right)
+        send(low, low, ("left", r), left)
+        send(low, low, ("right2", r), right)
+        send(top, top, ("left2", r), left)
 
     def send_offset(r):
         bown[r] = section(r, D).T
@@ -328,14 +347,16 @@
     half = D // 2
 
     def forward(r):
-        arrive(agat.at[before, r], ("right", r))
         part = agat.at[before, r, pl.ds(0, half), :]
+        arrive(part, ("right", r))
         send(part, part, ("far_right", r), right)
-        arrive(agat.at[after, r], ("left", r))
         part = agat.at[after, r, pl.ds(half, half), :]
+        arrive(part, ("left", r))
         send(part, part, ("far_left", r), left)
 
     def compose(r):
+        arrive(agat.at[before, r, pl.ds(half, half), :], ("right2", r))
+        arrive(agat.at[after, r, pl.ds(0, half), :], ("left2", r))
         arrive(agat.at[far, r, pl.ds(0, half), :], ("far_right", r))
         arrive(agat.at[far, r, pl.ds(half, half), :], ("far_left", r))
         steps = [split(agat[i, r]) for i in range(X)]
@@ -445,12 +466,16 @@
         for m in count:
             r, c = batch[m]
             res = dot3(leads[m], (xh[r, c], xl[r, c]))
-            ah, al = split(res[:, :D])
-            qah[r, spans[m], :] = ah
-            qal[r, spans[m], :] = al
-            ob[r, spans[m], :] = boths[m][:, D:] + res[:, D:]
+            qf = qs[m].astype(F32)
+            norm = lax.rsqrt(jnp.sum(qf * qf, axis=1, keepdims=True) + 1e-06)
+            qah[r, spans[m], :], qal[r, spans[m], :] = split(res[:, :D] * norm)
+            ob[r, spans[m], :] = (boths[m][:, D:] + res[:, D:]) * norm
+            g = gate_ref[r, spans[m], :].astype(F32)
+            amp[r, spans[m], :] = gain * (g / (1.0 + jnp.exp(-g)))
 
     compose(0)
+    take_gate.wait()
+    gain = gain_ref[...]
     second(group(0))
     compose(1)
     second(group(1))
@@ -459,8 +484,6 @@
     second(group(3))
     settle(1)
 
-    gain = gain_ref[...]
-    take_gate.wait()
     puts = []
     for r in range(2):
         for o in (1, 2, 3):
@@ -468,26 +491,21 @@
             arrive(sin.at[r, there, :], ("state", o, r))
         state = split(sin[r])
 
-        def last_loop(i, _):
-            spans = [pl.ds(pl.multiple_of((2 * i + j) * C, C), C) for j in range(2)]
+        for i in range(GROUPS):
+            spans = [pl.ds((i * GROUP + j) * C, C) for j in range(GROUP)]
             raws = [
                 ob[r, span, :] + dot3((qah[r, span, :], qal[r, span, :]), state, mm_t)
                 for span in spans
             ]
-            for j in range(2):
-                span = spans[j]
-                qf = qk[0, r, span, :].astype(F32)
-                raw = raws[j] * lax.rsqrt(jnp.sum(qf * qf, axis=1, keepdims=True) + 1e-06)
-                mean = jnp.sum(raw * raw, axis=1, keepdims=True) * (1.0 / D)
-                g = gate_ref[r, span, :].astype(F32)
-                silu = g / (1.0 + jnp.exp(-g))
-                out_ref[r, span, :] = (raw * lax.rsqrt(mean + 1e-06) * gain * silu).astype(BF16)
-            return 0
-
-        lax.fori_loop(0, chunks // 2, last_loop, 0)
-        put = pltpu.make_async_copy(out_ref.at[r], out_hbm.at[r], local_sem.at[3 + r])
-        put.start()
-        puts.append(put)
+            means = [jnp.sum(raw * raw, axis=1, keepdims=True) * (1.0 / D) for raw in raws]
+            for raw, mean, span in zip(raws, means, spans):
+                out_ref[r, span, :] = (raw * lax.rsqrt(mean + 1e-06) * amp[r, span, :]).astype(BF16)
+            part = pl.ds(i * GROUP * C, GROUP * C)
+            put = pltpu.make_async_copy(
+                out_ref.at[r, part, :], out_hbm.at[r, part, :], local_sem.at[3 + GROUPS * r + i]
+            )
+            put.start()
+            puts.append(put)
 
     for copy in swaps:
         copy.wait_send()
@@ -535,6 +553,7 @@
                 pltpu.VMEM((requests, length, D), BF16),
                 pltpu.VMEM((requests, length, D), BF16),
                 pltpu.VMEM((requests, length, D), F32),
+                pltpu.VMEM((requests, length, D), F32),
                 pltpu.VMEM((X, requests, D, D), F32),
                 pltpu.VMEM((requests, D, D), F32),
                 pltpu.VMEM((X, requests, block, D), F32),
@@ -550,7 +569,7 @@
                 pltpu.VMEM((requests, block, D), F32),
                 pltpu.VMEM((X, requests, block, D), F32),
                 pltpu.VMEM((requests, D, D), F32),
-                pltpu.SemaphoreType.DMA((5,)),
+                pltpu.SemaphoreType.DMA((3 + 2 * GROUPS,)),
                 pltpu.SemaphoreType.DMA((len(SEM),)),
                 pltpu.SemaphoreType.DMA((len(SEM),)),
             ],

time: 39.1 us -> 36.7 us (0.939)
  Pallas kernels: 37.1 us -> 34.7 us
    pallas_call x1, Pallas kernels: 37.1 us -> 34.7 us  [call(): pl.pallas_call(lambda *refs: kernel(chunks, *refs), out_shape=jax.ShapeDt...]
where the time goes in v4:
time: 36.7 us; the launch traced here: 36.5 us
  Pallas kernels  34.7 us (95%)
  local copies, waits for them, and re-layouts  1.87 us (5%)
    pallas_call x1, Pallas kernels, call(): pl.pallas_call(lambda *refs: kernel(chunks, *refs), out_shape=jax.ShapeDt...  34.7 us
    unnamed x1, local copies, waits for them, and re-layouts  1.87 us

profile of v4, /device:TPU:56, one launch (start us, length us, event | category | flops | bytes accessed | tf_op | source)
XLA Modules:
  0.0 36.5 jit_solution(2022987233340732813)
XLA Ops:
  0.0 34.7 %shard_map.64 = bf16[2,1024,128]{2,1,0:T(8,128)(2,1)} custom-call(bf16[2,1024,128]{2,1,0:T(8,128)(2,1)} %refs_0_.1, bf16[2,1024,128]{2,1,0:T(8,128)(2,1)} %refs_1_.1, bf16[2,1024,128]{2,1,0:T(8,128)(2,1)} %refs_2_.1, f32[2,8,128]{2,1,0:T(8,128)} %bitcast.3, f32[2,8,128]{2,1,0:T(8,128)} %bitcast.4, f32[1,128]{1,0:T(1,128)} %bitcast.5), custom_call_target="tpu_custom_call" | custom-call | tf_op jit(solution)/shard_map/pallas_call | solution.py:534
  34.7 1.9 %copy.8 = bf16[2,1024,128]{2,1,0:T(8,128)(2,1)} copy(bf16[2,1024,128]{2,1,0:T(8,128)(2,1)} %shard_map.64) | data formatting | bytes 1048576

commit v5 on v4

--- a/solution.py
+++ b/solution.py
@@ -360,16 +360,13 @@
         arrive(agat.at[far, r, pl.ds(0, half), :], ("far_right", r))
         arrive(agat.at[far, r, pl.ds(half, half), :], ("far_left", r))
         steps = [split(agat[i, r]) for i in range(X)]
-        lead = steps[0]
-        lead_h[r, 0], lead_l[r, 0] = lead
-        for i in range(1, X):
-            whole = dot3(steps[i], lead)
-            if i < X - 1:
-                lead = split(whole)
-                lead_h[r, i], lead_l[r, i] = lead
-            else:
-                comp[r] = whole
+        lead_h[r, 0], lead_l[r, 0] = steps[0]
+        lower = split(dot3(steps[1], steps[0]))
+        upper = split(dot3(steps[3], steps[2]))
+        comp[r] = dot3(upper, lower)
         push(gains, r)
+        lead_h[r, 1], lead_l[r, 1] = lower
+        lead_h[r, 2], lead_l[r, 2] = split(dot3(steps[2], lower))
         for o in (1, 2, 3):
             arrive(bgat.at[lax.rem(col + X - o, X), r], ("block", o, r))
         offset = bgat[0, r]
@@ -384,13 +381,13 @@
             return []
         return [
             remote(comp.at[r], ya.at[s - 1, r], ("gain", s, d, r), d * X + col)
-            for d in range(s + 1, X)
+            for d in reversed(range(s + 1, X))
         ]
 
     def offsets(r, s):
         return [
             remote(offs.at[r, X - 1], yb.at[s, r], ("offset", s, d, r), d * X + col)
-            for d in range(s + 1, X)
+            for d in reversed(range(s + 1, X))
         ]
 
     def push(copies, r):
@@ -479,8 +476,8 @@
     second(group(0))
     compose(1)
     second(group(1))
+    second(group(2))
     settle(0)
-    second(group(2))
     second(group(3))
     settle(1)
 

time: 36.7 us -> 36.6 us (level)
  no operation moved by 1% of the time
where the time goes in v5:
time: 36.6 us; the launch traced here: 36.4 us
  Pallas kernels  34.5 us (94%)
  local copies, waits for them, and re-layouts  1.87 us (5%)
    pallas_call x1, Pallas kernels, call(): pl.pallas_call(lambda *refs: kernel(chunks, *refs), out_shape=jax.ShapeDt...  34.5 us
    unnamed x1, local copies, waits for them, and re-layouts  1.87 us

profile of v5, /device:TPU:56, one launch (start us, length us, event | category | flops | bytes accessed | tf_op | source)
XLA Modules:
  0.0 36.4 jit_solution(4693589917948783822)
XLA Ops:
  0.0 34.5 %shard_map.64 = bf16[2,1024,128]{2,1,0:T(8,128)(2,1)} custom-call(bf16[2,1024,128]{2,1,0:T(8,128)(2,1)} %refs_0_.1, bf16[2,1024,128]{2,1,0:T(8,128)(2,1)} %refs_1_.1, bf16[2,1024,128]{2,1,0:T(8,128)(2,1)} %refs_2_.1, f32[2,8,128]{2,1,0:T(8,128)} %bitcast.3, f32[2,8,128]{2,1,0:T(8,128)} %bitcast.4, f32[1,128]{1,0:T(1,128)} %bitcast.5), custom_call_target="tpu_custom_call" | custom-call | tf_op jit(solution)/shard_map/pallas_call | solution.py:531
  34.5 1.9 %copy.8 = bf16[2,1024,128]{2,1,0:T(8,128)(2,1)} copy(bf16[2,1024,128]{2,1,0:T(8,128)(2,1)} %shard_map.64) | data formatting | bytes 1048576
